TPU v7x, 32 devices: a whole 2x2x4 slice. The times are simulated.
32 devices in a mesh: mem: 16 (over z, y, x), row: 2 (over core).
Axes of the slice: x: 2, y: 2, z: 4, core: 2. Of those that a mesh axis runs over, the one named last changes fastest.
Arguments:
- realization_stack: float32 [16, 5, 32, 256], P('mem', None, 'row'), may hold values from -6 to 6
- velocity: float32 [2, 32, 256], P(None, 'row'), may hold values from -0.25 to 0.25
- diffusion: float32 [5], replicated, may hold values from 0.04 to 0.12
- obs_cell: int32 [2048], replicated, may hold values from 0 to 40959
- obs_order: int32 [2048], replicated, may hold values from 0 to 2047, each once
- obs_value: float32 [2048], replicated, may hold values from -6 to 6
- obs_var: float32 [2048], replicated, may hold values from 0.2 to 2
- field_mask: int32 [5, 5], replicated, may hold values 0 or 1
Outputs:
- analysis: float32 [16, 5, 2, 16, 256], P(None, None, 'row', 'mem')
Inputs may be any that keep to these rules, and one draw needn't show every extreme that they name: `obs_cell`: a flat index field * 32 * 256 + row * 256 + column. `obs_order`: each of 0 to 2047 exactly once.
All inputs are finite; a program needn't handle non-finite values.
Results may differ from a plain program's by a relative error of at most 0.0003.
Values sent between devices are 32-bit elements; how exact they have to be, the bound alone decides.
No kernel may reach another device: no remote copies, remote signals or barrier semaphores. Data moves between devices by JAX's collectives and lax.ppermute only.
A program may use at most 64 MiB of HBM per device.

v0:
```python
import jax
import jax.numpy as jnp
from jax import lax
from jax.sharding import PartitionSpec as P

SUBSTEPS = 4
BATCHES = 2
LOC_HALF = 32


precise = lax.Precision.HIGHEST


def extended(shard, sides, width):
    for axis, dim in sides:
        count, length = (lax.axis_size(axis), shard.shape[dim])
        up = [(i, (i + 1) % count) for i in range(count - 1)]
        down = [(j, i) for i, j in up]
        last = lax.slice_in_dim(shard, length - width, length, axis=dim)
        initial = lax.slice_in_dim(shard, 0, width, axis=dim)
        before = lax.ppermute(last, axis, up)
        after = lax.ppermute(initial, axis, down)
        shard = jnp.concatenate([before, shard, after], axis=dim)
    return shard


def advance(padded, velocity, diffusion):
    spec_pad = ((0, 0),) * (padded.ndim - 1) + ((1, 1),)
    col_padded = jnp.pad(padded, spec_pad)
    centre = col_padded[..., 1:-1, 1:-1]
    north_cell = col_padded[..., :-2, 1:-1]
    south_cell = col_padded[..., 2:, 1:-1]
    west_cell = col_padded[..., 1:-1, :-2]
    east_cell = col_padded[..., 1:-1, 2:]
    along_col = velocity[0]
    along_row = velocity[1]
    spread = north_cell + south_cell + west_cell + east_cell - 4.0 * centre
    carried = (
        jnp.maximum(along_col, 0.0) * (centre - west_cell)
        + jnp.minimum(along_col, 0.0) * (east_cell - centre)
        + jnp.maximum(along_row, 0.0) * (centre - north_cell)
        + jnp.minimum(along_row, 0.0) * (south_cell - centre)
    )
    return centre + diffusion[:, None, None] * spread - carried


def gaspari(dist_sq):
    scaled = jnp.sqrt(dist_sq) / LOC_HALF
    clipped = jnp.maximum(scaled, 1.0)
    inner_part = (
        ((-0.25 * scaled + 0.5) * scaled + 0.625) * scaled - 5.0 / 3.0
    ) * scaled * scaled + 1.0
    outer_part = (
        ((((scaled / 12.0 - 0.5) * scaled + 0.625) * scaled + 5.0 / 3.0) * scaled - 5.0) * scaled
        + 4.0
        - 2.0 / (3.0 * clipped)
    )
    return jnp.where(scaled <= 1.0, inner_part, jnp.where(scaled <= 2.0, outer_part, 0.0))


def decode(flat_cells, total_rows, n_cols):
    field_ids = flat_cells // (total_rows * n_cols)
    row_ids = flat_cells // n_cols % total_rows
    col_ids = flat_cells % n_cols
    return (field_ids, row_ids, col_ids)


def innovations(priors, obs_values, obs_noise):
    members = priors.shape[0]
    average = jnp.mean(priors, axis=0)
    anomaly = priors - average
    spread = jnp.sum(anomaly * anomaly, axis=0) / (members - 1)
    variance_sum = spread + obs_noise
    root_sum = jnp.sqrt(variance_sum)
    shrink = 1.0 / (root_sum * (jnp.sqrt(obs_noise) + root_sum))
    adjust = (obs_values - average) / variance_sum - shrink * anomaly
    return (anomaly, adjust)


def regress(
    ensemble_now, base_row, obs_field, obs_row, obs_col, anomaly, adjust, field_mask, n_cols
):
    members, n_cells = ensemble_now.shape
    n_fields = field_mask.shape[0]
    per_field = n_cells // n_fields
    local_ids = lax.iota(jnp.int32, per_field)
    cell_row = (base_row + local_ids // n_cols).astype(jnp.float32)
    cell_col = (local_ids % n_cols).astype(jnp.float32)
    centred = ensemble_now - jnp.mean(ensemble_now, axis=0)
    mask_float = field_mask.astype(jnp.float32)
    total_obs = obs_field.shape[0]
    obs_block = min(256, total_obs)
    increment = jnp.zeros_like(ensemble_now)
    for offset in range(0, total_obs, obs_block):
        row_gap = cell_row[:, None] - obs_row[None, offset : offset + obs_block].astype(jnp.float32)
        col_gap = cell_col[:, None] - obs_col[None, offset : offset + obs_block].astype(jnp.float32)
        closeness = gaspari(row_gap * row_gap + col_gap * col_gap)
        field_hot = (
            obs_field[None, offset : offset + obs_block] == lax.iota(jnp.int32, n_fields)[:, None]
        ).astype(jnp.float32)
        allowed = jnp.dot(mask_float, field_hot, precision=precise)
        covariance = lax.dot_general(
            centred,
            anomaly[:, offset : offset + obs_block],
            (((0,), (0,)), ((), ())),
            precision=precise,
        )
        weights = (
            covariance.reshape(n_fields, per_field, obs_block)
            * (closeness[None] * allowed[:, None, :])
            / (members - 1)
        )
        increment = increment + lax.dot_general(
            adjust[:, offset : offset + obs_block],
            weights.reshape(n_cells, obs_block),
            (((1,), (1,)), ((), ())),
            precision=precise,
        )
    return ensemble_now + increment


def per_device(
    realization_stack, velocity, diffusion, obs_cell, obs_order, obs_value, obs_var, field_mask
):
    local_members = realization_stack.shape[0]
    n_fields = realization_stack.shape[1]
    rows_here = realization_stack.shape[2]
    n_cols = realization_stack.shape[3]
    n_mem = lax.axis_size("mem")
    n_slab = lax.axis_size("row")
    total_members = local_members * n_mem
    total_rows = rows_here * n_slab
    slab_index = lax.axis_index("row")
    member_index = lax.axis_index("mem")
    row_sub = rows_here // n_mem
    current = realization_stack
    for substep in range(SUBSTEPS):
        padded = extended(current, (("row", 2),), 1)
        current = advance(padded, velocity, diffusion)
    field_all, row_all, col_all = decode(obs_cell, total_rows, n_cols)
    batch_size = obs_cell.shape[0] // BATCHES
    layout = lax.all_to_all(current, "mem", split_axis=2, concat_axis=0, tiled=True)
    ensemble_now = layout.reshape(total_members, -1)
    base_row = slab_index * rows_here + member_index * row_sub
    for batch_num in range(BATCHES):
        picked = obs_order[batch_num * batch_size : (batch_num + 1) * batch_size]
        obs_field = field_all[picked]
        obs_row = row_all[picked]
        obs_col = col_all[picked]
        owned = ((obs_row >= base_row) & (obs_row < base_row + row_sub)).astype(jnp.float32)
        local_ids = (
            obs_field * row_sub * n_cols
            + jnp.clip(obs_row - base_row, 0, row_sub - 1) * n_cols
            + obs_col
        )
        partial_priors = jnp.take(ensemble_now, local_ids, axis=1) * owned[None, :]
        priors = lax.psum(partial_priors, ("mem", "row"))
        anomaly, adjust = innovations(priors, obs_value[picked], obs_var[picked])
        ensemble_now = regress(
            ensemble_now, base_row, obs_field, obs_row, obs_col, anomaly, adjust, field_mask, n_cols
        )
    return ensemble_now.reshape(total_members, n_fields, 1, row_sub, n_cols)


def solution(mesh):
    in_specs = (P("mem", None, "row", None), P(None, "row", None), P(), P(), P(), P(), P(), P())
    out_specs = P(None, None, "row", "mem", None)
    return jax.shard_map(
        per_device, mesh=mesh, in_specs=in_specs, out_specs=out_specs, check_vma=False
    )
```

profile of v0, /device:TPU:0, one launch (start us, length us, event | category | flops | bytes accessed | tf_op | source)
XLA Modules:
  0.0 403.0 jit_solution(6026265140585205028)
XLA Ops:
  7.5 1.3 collective-permute-start.1
  8.8 3.0 collective-permute-start
  13.3 6.1 %gather_fusion.8 = s32[1024]{0:T(1024)S(1)} fusion(s32[2048]{0:T(1024)S(1)} %get-tuple-element.33, s32[1024]{0:T(1024)S(1)} %get-tuple-element.28), kind=kCustom, calls=%fused_computation.10 | custom fusion | bytes 12288 | tf_op jit(solution)/shard_map/gather | solution.py:149
  19.4 6.2 %gather_fusion.7 = s32[1024]{0:T(1024)S(1)} fusion(s32[2048]{0:T(1024)S(1)} %get-tuple-element.32, s32[1024]{0:T(1024)S(1)} %get-tuple-element.28), kind=kCustom, calls=%fused_computation.9 | custom fusion | bytes 12288 | tf_op jit(solution)/shard_map/gather | solution.py:148
  25.6 6.2 %gather_fusion.3 = s32[1024]{0:T(1024)S(1)} fusion(s32[2048]{0:T(1024)S(1)} %get-tuple-element.33, s32[1024]{0:T(1024)S(1)} %get-tuple-element.29), kind=kCustom, calls=%fused_computation.5 | custom fusion | bytes 12288 | tf_op jit(solution)/shard_map/gather | solution.py:149
  31.8 6.2 %gather_fusion.2 = s32[1024]{0:T(1024)S(1)} fusion(s32[2048]{0:T(1024)S(1)} %get-tuple-element.32, s32[1024]{0:T(1024)S(1)} %get-tuple-element.29), kind=kCustom, calls=%fused_computation.4 | custom fusion | bytes 12288 | tf_op jit(solution)/shard_map/gather | solution.py:148
  37.9 6.2 %gather_fusion.1 = s32[1024]{0:T(1024)S(1)} fusion(s32[2048]{0:T(1024)S(1)} %get-tuple-element.34, s32[1024]{0:T(1024)S(1)} %get-tuple-element.29), kind=kCustom, calls=%fused_computation.3 | custom fusion | bytes 12288 | tf_op jit(solution)/shard_map/gather | solution.py:147
  44.1 6.2 %gather_fusion.6 = s32[1024]{0:T(1024)S(1)} fusion(s32[2048]{0:T(1024)S(1)} %get-tuple-element.34, s32[1024]{0:T(1024)S(1)} %get-tuple-element.28), kind=kCustom, calls=%fused_computation.8 | custom fusion | bytes 12288 | tf_op jit(solution)/shard_map/gather | solution.py:147
  51.1 3.7 fusion.25
  55.0 1.7 broadcast_multiply_fusion
  57.2 1.3 collective-permute-start.3
  58.5 3.0 collective-permute-start.2
  62.6 1.3 collective-permute-start.5
  63.9 3.0 collective-permute-start.4
  68.0 1.3 collective-permute-start.7
  69.3 3.0 collective-permute-start.6
  72.4 6.2 %gather_fusion = f32[1024]{0:T(1024)S(1)} fusion(f32[2048]{0:T(1024)S(1)} %copy-done, s32[1024]{0:T(1024)S(1)} %get-tuple-element.29), kind=kCustom, calls=%fused_computation.2 | custom fusion | bytes 12288 | tf_op jit(solution)/shard_map/gather | solution.py:158
  78.6 6.2 %gather_fusion.5 = f32[1024]{0:T(1024)S(1)} fusion(f32[2048]{0:T(1024)S(1)} %copy-done, s32[1024]{0:T(1024)S(1)} %get-tuple-element.28), kind=kCustom, calls=%fused_computation.7 | custom fusion | bytes 12288 | tf_op jit(solution)/shard_map/gather | solution.py:158
  84.7 6.2 %gather_fusion.4 = f32[1024]{0:T(1024)S(1)} fusion(f32[2048]{0:T(1024)S(1)} %copy-done.1, s32[1024]{0:T(1024)S(1)} %get-tuple-element.29), kind=kCustom, calls=%fused_computation.6 | custom fusion | bytes 12288 | tf_op jit(solution)/shard_map/gather | solution.py:158
  90.9 6.2 %gather_fusion.9 = f32[1024]{0:T(1024)S(1)} fusion(f32[2048]{0:T(1024)S(1)} %copy-done.1, s32[1024]{0:T(1024)S(1)} %get-tuple-element.28), kind=kCustom, calls=%fused_computation.11 | custom fusion | bytes 12288 | tf_op jit(solution)/shard_map/gather | solution.py:158
  98.0 8.3 %all-to-all-start = ((f32[1,5,16,256]{3,1,0,2:T(8,128)}), f32[1,5,16,256]{3,1,0,2:T(8,128)S(1)}, u32[]{:S(2)}, u32[]{:S(2)}) async-start(f32[1,5,16,256]{3,1,0,2:T(8,128)} %fusion.48), calls=%async_computation | async-start | bytes 262144 | tf_op jit(solution)/shard_map/all_to_all | solution.py:142
  106.4 7.7 %all-to-all-done = f32[1,5,16,256]{3,1,0,2:T(8,128)S(1)} async-done(((f32[1,5,16,256]{3,1,0,2:T(8,128)}), f32[1,5,16,256]{3,1,0,2:T(8,128)S(1)}, u32[]{:S(2)}, u32[]{:S(2)}) %all-to-all-start) | async-done | bytes 81952 | tf_op jit(solution)/shard_map/all_to_all | solution.py:142
  114.4 4.0 gather_fusion.10
  120.6 114.6 %all-reduce.7.cloned.1.call-done = f32[16,1024]{1,0:T(8,128)} async-done(((f32[16,1024]{1,0:T(8,128)}), f32[16,1024]{1,0:T(8,128)}) %all-reduce.7.cloned.1.call-update) | async-done | bytes 65552 | tf_op jit(solution)/shard_map/psum | solution.py:157
  247.1 4.2 %gather_fusion.11 = f32[1024,16]{1,0:T(8,128)} fusion(f32[16,1280]{0,1:T(8,128)S(1)} %copy.44, s32[1024]{0:T(1024)S(1)} %broadcast_clamp_fusion), kind=kCustom, calls=%fused_computation.1.clone | custom fusion | bytes 135168 | tf_op jit(solution)/shard_map/jit(_take)/gather | solution.py:156
  251.3 2.2 bitcast_multiply_fusion
  253.5 128.8 %all-reduce.9.cloned.1.call-done = f32[16,1024]{0,1:T(8,128)} async-done(((f32[16,1024]{0,1:T(8,128)}), f32[16,1024]{0,1:T(8,128)}) %all-reduce.9.cloned.1.call-update) | async-done | bytes 65552 | tf_op jit(solution)/shard_map/psum | solution.py:157
  383.5 1.4 multiply_reduce_fusion
  384.9 1.3 fusion
  391.7 1.3 convolution_add_fusion.2
  392.9 1.3 convolution_add_fusion.1
  394.2 1.3 fusion.4
  (102 shorter events, 28.5 us)
Async XLA Ops:
  6.5 65.8 %copy-start = (f32[2048]{0:T(1024)S(1)}, f32[2048]{0:T(1024)}, u32[]{:S(2)}) copy-start(f32[2048]{0:T(1024)} %param.15) | copy-start | bytes 24580
  7.5 49.4 %collective-permute-start.1 = (f32[1,5,1,256]{3,1,0,2:T(8,128)S(1)}, f32[1,5,1,256]{3,1,0,2:T(8,128)S(1)}, u32[]{:S(2)}, u32[]{:S(2)}) collective-permute-start(f32[1,5,1,256]{3,1,0,2:T(8,128)S(1)} %get-tuple-element.21), channel_id=1, source_target_pairs={{1,0},{3,2},{5,4},{7,6},{9,8},{11,10},{13,12},{15,14},{17,16},{19,... | collective-permute-start | bytes 15368 | tf_op jit(solution)/shard_map/ppermute | solution.py:22
  8.8 48.1 %collective-permute-start = (f32[1,5,1,256]{3,1,0,2:T(8,128)S(1)}, f32[1,5,1,256]{3,1,0,2:T(8,128)S(1)}, u32[]{:S(2)}, u32[]{:S(2)}) collective-permute-start(f32[1,5,1,256]{3,1,0,2:T(8,128)S(1)} %get-tuple-element.20), channel_id=1, source_target_pairs={{0,1},{2,3},{4,5},{6,7},{8,9},{10,11},{12,13},{14,15},{16,17},{18,... | collective-permute-start | bytes 15368 | tf_op jit(solution)/shard_map/ppermute | solution.py:21
  44.1 6.2 %copy-start.9 = (f32[2,16,256]{2,1,0:T(8,128)S(1)}, f32[2,16,256]{2,1,0:T(8,128)}, u32[]{:S(2)}) copy-start(f32[2,16,256]{2,1,0:T(8,128)} %param.11) | copy-start | bytes 98308
  44.1 6.3 %copy-start.8 = (s32[5,5]{1,0:T(8,128)S(1)}, s32[5,5]{1,0:T(8,128)}, u32[]{:S(2)}) copy-start(s32[5,5]{1,0:T(8,128)} %param.17) | copy-start | bytes 304
  55.0 2.0 copy-start.10
  57.2 4.5 %collective-permute-start.3 = (f32[1,5,1,256]{3,1,0,2:T(8,128)S(1)}, f32[1,5,1,256]{3,1,0,2:T(8,128)S(1)}, u32[]{:S(2)}, u32[]{:S(2)}) collective-permute-start(f32[1,5,1,256]{3,1,0,2:T(8,128)S(1)} %get-tuple-element.19), channel_id=1, source_target_pairs={{1,0},{3,2},{5,4},{7,6},{9,8},{11,10},{13,12},{15,14},{17,16},{19,... | collective-permute-start | bytes 15368 | tf_op jit(solution)/shard_map/ppermute | solution.py:22
  58.5 3.8 collective-permute-start.2
  62.6 4.5 %collective-permute-start.5 = (f32[1,5,1,256]{3,1,0,2:T(8,128)S(1)}, f32[1,5,1,256]{3,1,0,2:T(8,128)S(1)}, u32[]{:S(2)}, u32[]{:S(2)}) collective-permute-start(f32[1,5,1,256]{3,1,0,2:T(8,128)S(1)} %get-tuple-element.17), channel_id=1, source_target_pairs={{1,0},{3,2},{5,4},{7,6},{9,8},{11,10},{13,12},{15,14},{17,16},{19,... | collective-permute-start | bytes 15368 | tf_op jit(solution)/shard_map/ppermute | solution.py:22
  63.9 3.8 collective-permute-start.4
  68.0 29.0 %collective-permute-start.7 = (f32[1,5,1,256]{3,1,0,2:T(8,128)S(1)}, f32[1,5,1,256]{3,1,0,2:T(8,128)S(1)}, u32[]{:S(2)}, u32[]{:S(2)}) collective-permute-start(f32[1,5,1,256]{3,1,0,2:T(8,128)S(1)} %get-tuple-element.15), channel_id=1, source_target_pairs={{1,0},{3,2},{5,4},{7,6},{9,8},{11,10},{13,12},{15,14},{17,16},{19,... | collective-permute-start | bytes 15368 | tf_op jit(solution)/shard_map/ppermute | solution.py:22
  69.3 27.7 %collective-permute-start.6 = (f32[1,5,1,256]{3,1,0,2:T(8,128)S(1)}, f32[1,5,1,256]{3,1,0,2:T(8,128)S(1)}, u32[]{:S(2)}, u32[]{:S(2)}) collective-permute-start(f32[1,5,1,256]{3,1,0,2:T(8,128)S(1)} %get-tuple-element.14), channel_id=1, source_target_pairs={{0,1},{2,3},{4,5},{6,7},{8,9},{10,11},{12,13},{14,15},{16,17},{18,... | collective-permute-start | bytes 15368 | tf_op jit(solution)/shard_map/ppermute | solution.py:21
  78.6 6.2 %copy-start.1 = (f32[2048]{0:T(1024)S(1)}, f32[2048]{0:T(1024)}, u32[]{:S(2)}) copy-start(f32[2048]{0:T(1024)} %param.16) | copy-start | bytes 24580
  98.0 16.1 %all-to-all-start = ((f32[1,5,16,256]{3,1,0,2:T(8,128)}), f32[1,5,16,256]{3,1,0,2:T(8,128)S(1)}, u32[]{:S(2)}, u32[]{:S(2)}) async-start(f32[1,5,16,256]{3,1,0,2:T(8,128)} %fusion.48), calls=%async_computation | async-start | bytes 262144 | tf_op jit(solution)/shard_map/all_to_all | solution.py:142
  106.3 128.8 %all-reduce.7.cloned.1.call-start = ((), (), s32[]{:S(2)}) async-start(), calls=%async_computation.1 | async-start | bytes 131072 | tf_op jit(solution)/shard_map/psum | solution.py:157
  118.4 118.5 %copy-start.7 = (f32[256,256]{1,0:T(8,128)S(1)}, f32[256,256]{1,0:T(8,128)}, u32[]{:S(2)}) copy-start(f32[256,256]{1,0:T(8,128)} %get-tuple-element.68) | copy-start | bytes 786436
  120.3 261.9 %all-reduce.9.cloned.1.call-start = ((), (), s32[]{:S(2)}) async-start(), calls=%async_computation.2 | async-start | bytes 1048576 | tf_op jit(solution)/shard_map/psum | solution.py:157
  236.9 2.5 copy-start.6
  239.4 2.5 copy-start.5
  241.9 2.5 copy-start.4
  386.2 1.3 copy-start.3
  387.5 1.3 copy-start.2
Sparse Core Ops, SparseCore 0:
  120.5 114.6 all-reduce.6
  253.6 128.6 all-reduce.8
where the time goes:
time: 404 us; the launch traced here: 403 us
  waiting for transfers between devices  253 us (63%)
  local copies, waits for them, and re-layouts  73.4 us (18%)
  starting transfers between devices  25.9 us (6%)
  matrix products  20.7 us (5%)
  other arithmetic  16.5 us (4%)
  between operations  14.1 us (3%)
    psum x2, waiting for transfers between devices, per_device(): priors = lax.psum(partial_priors, ('mem', 'row'))  243 us
    gather x4, local copies, waits for them, and re-layouts, per_device(): anomaly, adjust = innovations(priors, obs_value[picked], obs_var[picked])  24.6 us
    gather x2, local copies, waits for them, and re-layouts, per_device(): obs_row = row_all[picked]  12.3 us
    gather x2, local copies, waits for them, and re-layouts, per_device(): obs_field = field_all[picked]  12.3 us
    gather x2, local copies, waits for them, and re-layouts, per_device(): obs_col = col_all[picked]  12.3 us
    ppermute x4, starting transfers between devices, extended(): before = lax.ppermute(last, axis, up)  12.1 us
    dot_general x8, matrix products, regress(): lax.dot_general(centred, anomaly[:, offset:offset + obs_block], (((0,), (...  9.99 us
    dot_general x8, matrix products, regress(): lax.dot_general(adjust[:, offset:offset + obs_block], weights.reshape(n_c...  9.76 us
  transfers between devices with their start and end apart: 11, of which 5 were waited for; matrix products, arithmetic and copies ran while one was open for 17% of the time, Pallas kernels for 0%

commit v1 on v0

--- a/solution.py
+++ b/solution.py
@@ -1,6 +1,10 @@
+import functools
+
 import jax
 import jax.numpy as jnp
 from jax import lax
+from jax.experimental import pallas as pl
+from jax.experimental.pallas import tpu as pltpu
 from jax.sharding import PartitionSpec as P
 
 SUBSTEPS = 4
@@ -119,6 +123,377 @@
     return ensemble_now + increment
 
 
+LANES = 128
+MEGA = 1 << 20
+
+
+def split_two(x):
+    high = x.astype(jnp.bfloat16)
+    low = (x - high.astype(jnp.float32)).astype(jnp.bfloat16)
+    return high, low
+
+
+def split_three(x):
+    high = x.astype(jnp.bfloat16)
+    rest = x - high.astype(jnp.float32)
+    mid = rest.astype(jnp.bfloat16)
+    low = (rest - mid.astype(jnp.float32)).astype(jnp.bfloat16)
+    return high, mid, low
+
+
+def bdot(a, b):
+    return jnp.dot(a, b, preferred_element_type=jnp.float32)
+
+
+def log2(n):
+    return n.bit_length() - 1
+
+
+def prep_kernel(order_ref, cell_ref, value_ref, var_ref, info_ref, infot_ref, *, total_rows, n_cols):
+    table_rows = cell_ref.shape[0]
+    order = order_ref[...]
+    n_obs = order.shape[1]
+    table = jnp.concatenate(
+        [cell_ref[...].astype(jnp.float32), value_ref[...], var_ref[...]], axis=0
+    )
+    parts = jnp.concatenate(split_three(table), axis=0)
+    lane_hot = (
+        lax.broadcasted_iota(jnp.int32, (LANES, n_obs), 0) == (order & (LANES - 1))
+    ).astype(jnp.float32).astype(jnp.bfloat16)
+    found = bdot(parts, lane_hot)
+    size = 3 * table_rows
+    found = (found[:size] + found[size : 2 * size]) + found[2 * size :]
+    row_hot = lax.broadcasted_iota(jnp.int32, (table_rows, n_obs), 0) == (order >> log2(LANES))
+
+    def take(i):
+        rows = found[i * table_rows : (i + 1) * table_rows]
+        return jnp.sum(jnp.where(row_hot, rows, 0.0), axis=0, keepdims=True)
+
+    cell = take(0).astype(jnp.int32)
+    strip = cell >> log2(n_cols)
+    field = strip >> log2(total_rows)
+    row = strip & (total_rows - 1)
+    col = cell & (n_cols - 1)
+    as_float = lambda x: x.astype(jnp.float32)
+    zero = jnp.zeros((1, n_obs), jnp.float32)
+    info = jnp.concatenate(
+        [as_float(field), as_float(row), as_float(col), take(1), take(2), as_float(strip), zero, zero],
+        axis=0,
+    )
+    info_ref[...] = info
+    infot_ref[...] = info.T
+
+
+def forecast_kernel(
+    place_ref, diffusion_ref, own_ref, other_ref, vel_own_ref, vel_other_ref, info_ref,
+    send_ref, field_buf, vel_buf, prior_buf,
+):
+    n_fields, n_rows, n_cols = field_buf.shape
+    half = n_rows // 2
+    n_dest = half
+    chunk = send_ref.shape[0] // n_dest
+    mine = pl.multiple_of(place_ref[0] * half, half)
+    theirs = pl.multiple_of((1 - place_ref[0]) * half, half)
+    vel_buf[:, pl.ds(mine, half), :] = vel_own_ref[...]
+    vel_buf[:, pl.ds(theirs, half), :] = vel_other_ref[...]
+    field_buf[:, pl.ds(mine, half), :] = own_ref[0]
+    field_buf[:, pl.ds(theirs, half), :] = other_ref[0]
+    u = vel_buf[0]
+    v = vel_buf[1]
+    row = lax.broadcasted_iota(jnp.int32, (n_rows, n_cols), 0)
+    col = lax.broadcasted_iota(jnp.int32, (n_rows, n_cols), 1)
+    u_pos, u_neg = jnp.maximum(u, 0.0), jnp.minimum(u, 0.0)
+    v_pos, v_neg = jnp.maximum(v, 0.0), jnp.minimum(v, 0.0)
+    outflow = (u_neg - u_pos) + (v_neg - v_pos)
+    for f in range(n_fields):
+        kappa = diffusion_ref[f]
+        k_c = (1.0 - 4.0 * kappa) + outflow
+        k_n = jnp.where(row == 0, 0.0, kappa + v_pos)
+        k_s = jnp.where(row == n_rows - 1, 0.0, kappa - v_neg)
+        k_w = jnp.where(col == 0, 0.0, kappa + u_pos)
+        k_e = jnp.where(col == n_cols - 1, 0.0, kappa - u_neg)
+        c = field_buf[f]
+        for _ in range(SUBSTEPS):
+            c = (
+                (c * k_c + pltpu.roll(c, 1, 0) * k_n)
+                + (pltpu.roll(c, n_rows - 1, 0) * k_s + pltpu.roll(c, 1, 1) * k_w)
+                + pltpu.roll(c, n_cols - 1, 1) * k_e
+            )
+        field_buf[f] = c
+    whole = field_buf[...].reshape(n_fields * n_rows, n_cols)
+    strips = n_fields * n_rows
+    parts = jnp.concatenate(split_three(whole), axis=0)
+    n_obs = info_ref.shape[1]
+    width = 2 * LANES
+    strip_ids = lax.broadcasted_iota(jnp.int32, (strips, width), 0)
+    col_ids = lax.broadcasted_iota(jnp.int32, (n_cols, width), 0)
+    for q in range(n_obs // width):
+        cols = info_ref[2:3, q * width : (q + 1) * width].astype(jnp.int32)
+        strip = info_ref[5:6, q * width : (q + 1) * width].astype(jnp.int32)
+        hot = (col_ids == cols).astype(jnp.float32).astype(jnp.bfloat16)
+        found = bdot(parts, hot)
+        found = (found[:strips] + found[strips : 2 * strips]) + found[2 * strips :]
+        values = jnp.sum(jnp.where(strip_ids == strip, found, 0.0), axis=0, keepdims=True)
+        for h in range(width // LANES):
+            at = q * (width // LANES) + h
+            prior_buf[at : at + 1, :] = values[:, h * LANES : (h + 1) * LANES]
+    priors = prior_buf[...]
+    lead = chunk - n_obs // LANES
+    for d in range(n_dest):
+        send_ref[d * chunk + lead : (d + 1) * chunk, :] = priors
+    pieces = n_cols // LANES
+    for f in range(n_fields):
+        rows = field_buf[f, pl.ds(mine, half), :]
+        for h in range(pieces):
+            send_ref[pl.ds(f * pieces + h, n_dest, stride=chunk), :] = rows[
+                :, h * LANES : (h + 1) * LANES
+            ]
+    for i in range(n_fields * pieces, lead):
+        send_ref[pl.ds(i, n_dest, stride=chunk), :] = jnp.zeros((n_dest, LANES), jnp.float32)
+
+
+def closeness_of(dist_sq):
+    inverse = lax.rsqrt(jnp.maximum(dist_sq, 1e-12))
+    z = dist_sq * inverse
+    half_sq = 0.5 * dist_sq
+    inner = 1.0 + dist_sq * ((half_sq - 5.0 / 3.0) + z * (0.625 - 0.5 * half_sq))
+    outer = (
+        (4.0 + dist_sq * (5.0 / 3.0 - half_sq))
+        + z * (dist_sq * (dist_sq * (1.0 / 12.0) + 0.625) - 5.0)
+        - (2.0 / 3.0) * inverse
+    )
+    return jnp.where(dist_sq <= 1.0, inner, jnp.where(dist_sq <= 4.0, outer, 0.0))
+
+
+def loc_kernel(
+    place_ref, mask_ref, info_ref, infot_ref,
+    pair_hi_ref, pair_lo_ref, cell_hi_ref, cell_lo_ref, allow_buf,
+):
+    n_obs = info_ref.shape[1]
+    batch = n_obs // BATCHES
+    n_fields = mask_ref.shape[0]
+    n_cols = cell_hi_ref.shape[1]
+    scale = 1.0 / LOC_HALF
+    step = 16
+    field_j = info_ref[0:1, batch:].astype(jnp.int32)
+    hot_j = (lax.broadcasted_iota(jnp.int32, (8, n_obs - batch), 0) == field_j).astype(jnp.float32)
+    field_k = infot_ref[0:batch, 0:1].astype(jnp.int32)
+    lane = lax.broadcasted_iota(jnp.int32, (1, 8), 1)
+    reach = jnp.zeros((batch, 8), jnp.float32)
+    for b in range(n_fields):
+        line = jnp.zeros((1, 8), jnp.float32)
+        for a in range(n_fields):
+            line = jnp.where(lane == a, mask_ref[a, b].astype(jnp.float32), line)
+        reach = jnp.where(field_k == b, line, reach)
+    allow_buf[...] = bdot(reach.astype(jnp.bfloat16), hot_j.astype(jnp.bfloat16))
+
+    half = 512
+
+    def pair_body(i, carry):
+        at = pl.multiple_of(i * step, step)
+        row_k = infot_ref[pl.ds(at, step), 1:2] * scale
+        col_k = infot_ref[pl.ds(at, step), 2:3] * scale
+        for h in range((n_obs - batch) // half):
+            here = slice(h * half, (h + 1) * half)
+            there = slice(batch + h * half, batch + (h + 1) * half)
+            d_row = info_ref[1:2, there] * scale - row_k
+            d_col = info_ref[2:3, there] * scale - col_k
+            loc = closeness_of(d_row * d_row + d_col * d_col) * allow_buf[pl.ds(at, step), here]
+            high, low = split_two(loc)
+            pair_hi_ref[pl.ds(at, step), here] = high
+            pair_lo_ref[pl.ds(at, step), here] = low
+        return carry
+
+    lax.fori_loop(0, batch // step, pair_body, 0)
+
+    own_row = place_ref[1].astype(jnp.float32) * scale
+    col_j = lax.broadcasted_iota(jnp.int32, (step, n_cols), 1).astype(jnp.float32) * scale
+
+    def cell_body(i, carry):
+        for h in range(2):
+            at = pl.multiple_of(i * (2 * step) + h * step, step)
+            d_row = infot_ref[pl.ds(at, step), 1:2] * scale - own_row
+            d_col = col_j - infot_ref[pl.ds(at, step), 2:3] * scale
+            high, low = split_two(closeness_of(d_row * d_row + d_col * d_col))
+            cell_hi_ref[pl.ds(at, step), :] = high
+            cell_lo_ref[pl.ds(at, step), :] = low
+        return carry
+
+    lax.fori_loop(0, n_obs // (2 * step), cell_body, 0)
+
+
+def member_roll(x, shift):
+    shift = shift % x.shape[0]
+    return pltpu.roll(x, shift, 0) if shift else x
+
+
+def factors(priors, value, var):
+    members = priors.shape[0]
+    average = jnp.sum(priors, axis=0, keepdims=True) * (1.0 / members)
+    anomaly = priors - average
+    variance = jnp.sum(anomaly * anomaly, axis=0, keepdims=True) * (1.0 / (members - 1)) + var
+    root = jnp.sqrt(variance)
+    shrunk = anomaly * (1.0 / ((members - 1) * (root * (jnp.sqrt(var) + root))))
+    rows = [shrunk * member_roll(anomaly, -d) for d in range(members // 2 + 1)]
+    rows.append(anomaly * ((value - average) / ((members - 1) * variance)))
+    return rows
+
+
+def combined(state, sums):
+    members = state.shape[0]
+    centred = state - jnp.sum(state, axis=0, keepdims=True) * (1.0 / members)
+    offsets = members // 2
+    block = lambda d: sums[d * members : (d + 1) * members]
+    move = centred * block(0) + member_roll(centred, -offsets) * block(offsets)
+    for d in range(1, offsets):
+        move = move + member_roll(centred, -d) * block(d)
+        move = move + member_roll(centred * block(d), d)
+    shift = jnp.sum(centred * block(offsets + 1), axis=0, keepdims=True)
+    return state + (shift - move)
+
+
+def update_kernel(
+    mask_ref, recv_ref, info_ref, pair_hi_ref, pair_lo_ref, cell_hi_ref, cell_lo_ref,
+    out_ref, fac_buf, *, members,
+):
+    n_obs = info_ref.shape[1]
+    batch = n_obs // BATCHES
+    n_fields = mask_ref.shape[0]
+    chunk = recv_ref.shape[0] // members
+    per_chunk = n_obs // LANES
+    lead = chunk - per_chunk
+    pieces = cell_hi_ref.shape[1] // LANES
+    size = fac_buf.shape[0] // 2
+
+    def member_row(i):
+        return recv_ref[pl.ds(i, members, stride=chunk), :]
+
+    state = [
+        jnp.concatenate([member_row(f * pieces + h) for h in range(pieces)], axis=1)
+        for f in range(n_fields)
+    ]
+    priors = jnp.concatenate([member_row(lead + q) for q in range(per_chunk)], axis=1)
+    upcoming = priors[:, batch:]
+    current = priors[:, :batch]
+    for b in range(BATCHES):
+        span = slice(b * batch, (b + 1) * batch)
+        rows = factors(current, info_ref[3:4, span], info_ref[4:5, span])
+        for i, r in enumerate(rows):
+            high, low = split_two(r)
+            fac_buf[i * members : (i + 1) * members, :] = high
+            fac_buf[size + i * members : size + (i + 1) * members, :] = low
+        if b == 0:
+            first = bdot(fac_buf[...], pair_hi_ref[...])
+            sums = (first[:size] + first[size:]) + bdot(fac_buf[:size, :], pair_lo_ref[...])
+            current = combined(upcoming, sums)
+        obs_field = info_ref[0:1, span].astype(jnp.int32)
+        for f in range(n_fields):
+            open_to = jnp.zeros((1, batch), jnp.float32)
+            for a in range(n_fields):
+                open_to = jnp.where(obs_field == a, mask_ref[f, a].astype(jnp.float32), open_to)
+            masked = fac_buf[...] * open_to.astype(jnp.bfloat16)
+            first = bdot(masked, cell_hi_ref[span, :])
+            sums = (first[:size] + first[size:]) + bdot(masked[:size], cell_lo_ref[span, :])
+            state[f] = combined(state[f], sums)
+    for f in range(n_fields):
+        out_ref[:, f, :] = state[f]
+
+
+def vmem_spec():
+    return pl.BlockSpec(memory_space=pltpu.VMEM)
+
+
+def smem_spec():
+    return pl.BlockSpec(memory_space=pltpu.SMEM)
+
+
+def quick_device(
+    realization_stack, velocity, diffusion, obs_cell, obs_order, obs_value, obs_var, field_mask
+):
+    _, n_fields, rows_here, n_cols = realization_stack.shape
+    n_mem = lax.axis_size("mem")
+    total_rows = 2 * rows_here
+    n_obs = obs_cell.shape[0]
+    batch = n_obs // BATCHES
+    slab_index = lax.axis_index("row")
+    own_row = slab_index * rows_here + lax.axis_index("mem")
+    place = jnp.stack([slab_index, own_row]).astype(jnp.int32)
+    params = pltpu.CompilerParams(vmem_limit_bytes=40 * MEGA)
+    shape = jax.ShapeDtypeStruct
+    swap = [(0, 1), (1, 0)]
+    other = lax.ppermute(realization_stack, "row", swap)
+    vel_other = lax.ppermute(velocity, "row", swap)
+    table = (n_obs // LANES, LANES)
+    info, infot = pl.pallas_call(
+        functools.partial(prep_kernel, total_rows=total_rows, n_cols=n_cols),
+        out_shape=(shape((8, n_obs), jnp.float32), shape((n_obs, 8), jnp.float32)),
+        in_specs=[vmem_spec()] * 4,
+        out_specs=(vmem_spec(), vmem_spec()),
+        compiler_params=params,
+        name="prep",
+    )(
+        obs_order.reshape(1, n_obs),
+        obs_cell.reshape(table),
+        obs_value.reshape(table),
+        obs_var.reshape(table),
+    )
+    chunk = -(-(n_fields * n_cols + n_obs) // (8 * LANES)) * 8
+    send = pl.pallas_call(
+        forecast_kernel,
+        out_shape=shape((n_mem * chunk, LANES), jnp.float32),
+        in_specs=[smem_spec(), smem_spec()] + [vmem_spec()] * 5,
+        out_specs=vmem_spec(),
+        scratch_shapes=[
+            pltpu.VMEM((n_fields, total_rows, n_cols), jnp.float32),
+            pltpu.VMEM((2, total_rows, n_cols), jnp.float32),
+            pltpu.VMEM((n_obs // LANES, LANES), jnp.float32),
+        ],
+        compiler_params=params,
+        name="forecast",
+    )(place, diffusion, realization_stack, other, velocity, vel_other, info)
+    recv = lax.all_to_all(send, "mem", split_axis=0, concat_axis=0, tiled=True)
+    locs = pl.pallas_call(
+        loc_kernel,
+        out_shape=(
+            shape((batch, n_obs - batch), jnp.bfloat16),
+            shape((batch, n_obs - batch), jnp.bfloat16),
+            shape((n_obs, n_cols), jnp.bfloat16),
+            shape((n_obs, n_cols), jnp.bfloat16),
+        ),
+        in_specs=[smem_spec(), smem_spec(), vmem_spec(), vmem_spec()],
+        out_specs=(vmem_spec(),) * 4,
+        scratch_shapes=[pltpu.VMEM((batch, n_obs - batch), jnp.float32)],
+        compiler_params=params,
+        name="localize",
+    )(place, field_mask, info, infot)
+    rows = n_mem * (n_mem // 2 + 2)
+    out = pl.pallas_call(
+        functools.partial(update_kernel, members=n_mem),
+        out_shape=shape((n_mem, n_fields, n_cols), jnp.float32),
+        in_specs=[smem_spec()] + [vmem_spec()] * 6,
+        out_specs=vmem_spec(),
+        scratch_shapes=[pltpu.VMEM((2 * rows, batch), jnp.bfloat16)],
+        compiler_params=params,
+        name="update",
+    )(field_mask, recv, info, *locs)
+    return out.reshape(n_mem, n_fields, 1, 1, n_cols)
+
+
+def is_quick(realization_stack, obs_cell, n_mem, n_slab):
+    local_members, n_fields, rows_here, n_cols = realization_stack.shape
+    powers = all(n & (n - 1) == 0 for n in (rows_here, n_cols))
+    return (
+        n_slab == 2
+        and local_members == 1
+        and n_mem == rows_here == 16
+        and n_fields <= 8
+        and powers
+        and n_cols % LANES == 0
+        and obs_cell.shape[0] == 8 * n_cols
+        and BATCHES == 2
+    )
+
+
 def per_device(
     realization_stack, velocity, diffusion, obs_cell, obs_order, obs_value, obs_var, field_mask
 ):
@@ -130,6 +505,10 @@
     n_slab = lax.axis_size("row")
     total_members = local_members * n_mem
     total_rows = rows_here * n_slab
+    if is_quick(realization_stack, obs_cell, n_mem, n_slab):
+        return quick_device(
+            realization_stack, velocity, diffusion, obs_cell, obs_order, obs_value, obs_var, field_mask
+        )
     slab_index = lax.axis_index("row")
     member_index = lax.axis_index("mem")
     row_sub = rows_here // n_mem

time: 404 us -> 49.7 us (0.12)
  waiting for transfers between devices: 253 us -> 0.01 us
  local copies, waits for them, and re-layouts: 73.4 us -> 13.8 us
  Pallas kernels: 0 us -> 26.2 us
  matrix products: 20.7 us -> 0 us
  starting transfers between devices: 25.9 us -> 8.82 us
  other arithmetic: 16.5 us -> 0.07 us
  between operations: 14.1 us -> 0.09 us
    psum x2 -> x0, waiting for transfers between devices: 243 us -> none  [per_device(): priors = lax.psum(partial_priors, ('mem', 'row'))]
    gather x13 -> x0, local copies, waits for them, and re-layouts: 71 us -> none  [the longest x4 24.6 us: per_device(): anomaly, adjust = innovations(priors, obs_value[picked], obs_var[picked])]
    pallas_call x0 -> x4, Pallas kernels: none -> 26.2 us  [the longest x1 18.5 us: quick_device(): pl.pallas_call(loc_kernel, out_shape=(shape((batch, n_obs - batch), jnp.b...]
    dot_general x24 -> x0, matrix products: 20.7 us -> none  [the longest x8 9.99 us: regress(): lax.dot_general(centred, anomaly[:, offset:offset + obs_block], (((0,), (...]
    ppermute x8 -> x2, starting transfers between devices: 17.3 us -> 0.52 us  [the longest x1 0.45 us: quick_device(): other = lax.ppermute(realization_stack, 'row', swap)]
    unnamed x24 -> x30, local copies, waits for them, and re-layouts: 1.18 us -> 13.1 us
    all_to_all x1, waiting for transfers between devices: 7.73 us -> 0.01 us  [quick_device(): recv = lax.all_to_all(send, 'mem', split_axis=0, concat_axis=0, tiled=True)]
    mul x4 -> x0, other arithmetic: 4.79 us -> none  [the longest x2 2.82 us: per_device(): partial_priors = jnp.take(ensemble_now, local_ids, axis=1) * owned[None, :]]
  transfers between devices with their start and end apart: 11 -> 3, of which waited for: 5 -> 0; matrix products, arithmetic and copies ran while one was open for 17% -> 0% of each run, Pallas kernels for 0% -> 39%
where the time goes in v1:
time: 49.7 us; the launch traced here: 49.1 us
  Pallas kernels  26.2 us (53%)
  local copies, waits for them, and re-layouts  13.8 us (28%)
  starting transfers between devices  8.82 us (18%)
    pallas_call x1, Pallas kernels, quick_device(): pl.pallas_call(loc_kernel, out_shape=(shape((batch, n_obs - batch), jnp.b...  18.5 us
    unnamed x30, local copies, waits for them, and re-layouts  13.1 us
    all_to_all x1, starting transfers between devices, quick_device(): recv = lax.all_to_all(send, 'mem', split_axis=0, concat_axis=0, tiled=True)  8.31 us
    pallas_call x1, Pallas kernels, quick_device(): pl.pallas_call(functools.partial(update_kernel, members=n_mem), out_shape...  4.69 us
    pallas_call x1, Pallas kernels, quick_device(): pl.pallas_call(forecast_kernel, out_shape=shape((n_mem * chunk, LANES), j...  2.45 us
  transfers between devices with their start and end apart: 3, of which 0 were waited for; matrix products, arithmetic and copies ran while one was open for 0% of the time, Pallas kernels for 39%

profile of v1, /device:TPU:0, one launch (start us, length us, event | category | flops | bytes accessed | tf_op | source)
XLA Modules:
  0.0 49.1 jit_solution(13813647896936252358)
XLA Ops:
  0.0 0.0 copy-start.9
  0.0 0.5 collective-permute-start
  0.5 0.1 collective-permute-start.1
  0.5 0.1 pad_add_fusion.place_ref
  0.6 0.7 %copy-done.10 = s32[2048]{0:T(1024)S(1)} copy-done((s32[2048]{0:T(1024)S(1)}, s32[2048]{0:T(1024)}, u32[]{:S(2)}) %copy-start.10) | copy-done | bytes 8216
  1.3 0.0 copy-start.11
  1.3 0.7 %copy-done.11 = s32[2048]{0:T(1024)S(1)} copy-done((s32[2048]{0:T(1024)S(1)}, s32[2048]{0:T(1024)}, u32[]{:S(2)}) %copy-start.11) | copy-done | bytes 8216
  2.0 0.7 %copy-done.12 = f32[2048]{0:T(1024)S(1)} copy-done((f32[2048]{0:T(1024)S(1)}, f32[2048]{0:T(1024)}, u32[]{:S(2)}) %copy-start.12) | copy-done | bytes 8216
  2.7 0.7 %copy-done.13 = f32[2048]{0:T(1024)S(1)} copy-done((f32[2048]{0:T(1024)S(1)}, f32[2048]{0:T(1024)}, u32[]{:S(2)}) %copy-start.13) | copy-done | bytes 8216
  3.4 0.5 %prep.1 = (f32[8,2048]{1,0:T(8,128)S(1)}, f32[2048,8]{1,0:T(8,128)S(1)}) custom-call(s32[1,2048]{1,0:T(1,128)S(1)} %bitcast.11, s32[16,128]{1,0:T(8,128)S(1)} %bitcast.12, f32[16,128]{1,0:T(8,128)S(1)} %bitcast.13, f32[16,128]{1,0:T(8,128)S(1)} %bitcast.14), custom_call_target="tpu_custom_call" | custom-call | tf_op jit(solution)/shard_map/prep/pallas_call | solution.py:427
  3.9 0.0 collective-permute-done.1.vel_other_ref
  3.9 0.0 collective-permute-done.other_ref
  4.0 0.0 copy-start.6
  4.0 0.9 %copy-done.6 = f32[1,5,16,256]{3,2,1,0:T(8,128)S(1)} copy-done((f32[1,5,16,256]{3,2,1,0:T(8,128)S(1)}, f32[1,5,16,256]{3,2,1,0:T(8,128)}, u32[]{:S(2)}) %copy-start.6) | copy-done | bytes 81944
  4.8 0.8 %copy-done.7 = f32[2,16,256]{2,1,0:T(8,128)S(1)} copy-done((f32[2,16,256]{2,1,0:T(8,128)S(1)}, f32[2,16,256]{2,1,0:T(8,128)}, u32[]{:S(2)}) %copy-start.7) | copy-done | bytes 32792
  5.6 0.7 %copy-done.14 = f32[5]{0:T(128)S(1)} copy-done((f32[5]{0:T(128)S(1)}, f32[5]{0:T(128)}, u32[]{:S(2)}) %copy-start.14) | copy-done | bytes 44
  6.3 2.5 %forecast.1 = f32[512,128]{1,0:T(8,128)} custom-call(s32[2]{0:T(128)S(1)} %pad_add_fusion.place_ref, f32[5]{0:T(128)S(1)} %copy-done.14, f32[1,5,16,256]{3,2,1,0:T(8,128)S(1)} %copy-done.6, f32[1,5,16,256]{3,2,1,0:T(8,128)S(1)} %collective-permute-done.other_ref, f32[2,16,256]{2,1,0:T(8,128)S(1)} %copy-done.7, ...), custom_call_target="tpu_custom_call" | custom-call | tf_op jit(solution)/shard_map/forecast/pallas_call | solution.py:441
  8.7 8.3 %all-to-all-start = ((f32[16,32,128]{2,1,0:T(8,128)}), f32[16,32,128]{2,1,0:T(8,128)S(1)}, u32[]{:S(2)}, u32[]{:S(2)}) async-start(f32[16,32,128]{2,1,0:T(8,128)} %bitcast.6), calls=%async_computation | async-start | bytes 524288 | tf_op jit(solution)/shard_map/all_to_all | solution.py:454
  17.0 0.0 copy-start.8
  17.0 0.7 %copy-done.8 = s32[5,5]{1,0:T(8,128)S(1)} copy-done((s32[5,5]{1,0:T(8,128)S(1)}, s32[5,5]{1,0:T(8,128)}, u32[]{:S(2)}) %copy-start.8) | copy-done | bytes 124
  17.7 18.5 %localize.1 = (bf16[1024,1024]{1,0:T(8,128)(2,1)S(1)}, bf16[1024,1024]{1,0:T(8,128)(2,1)S(1)}, bf16[2048,256]{1,0:T(8,128)(2,1)S(1)}, bf16[2048,256]{1,0:T(8,128)(2,1)S(1)}) custom-call(s32[2]{0:T(128)S(1)} %pad_add_fusion.place_ref, s32[5,5]{1,0:T(8,128)S(1)} %copy-done.8, f32[8,2048]{1,0:T(8,128)S(1)} %get-tuple-element.11.info_ref, ...), custom_call_target="tpu_custom_call" | custom-call | tf_op jit(solution)/shard_map/localize/pallas_call | solution.py:455
  36.3 0.0 copy-start
  36.3 1.3 %copy-done = bf16[1024,1024]{1,0:T(8,128)(2,1)} copy-done((bf16[1024,1024]{1,0:T(8,128)(2,1)}, bf16[1024,1024]{1,0:T(8,128)(2,1)S(1)}, u32[]{:S(2)}) %copy-start) | copy-done | bytes 2097176
  37.6 1.0 %copy-done.2 = bf16[2048,256]{1,0:T(8,128)(2,1)} copy-done((bf16[2048,256]{1,0:T(8,128)(2,1)}, bf16[2048,256]{1,0:T(8,128)(2,1)S(1)}, u32[]{:S(2)}) %copy-start.2) | copy-done | bytes 1048600
  38.6 1.0 %copy-done.4 = bf16[2048,256]{1,0:T(8,128)(2,1)} copy-done((bf16[2048,256]{1,0:T(8,128)(2,1)}, bf16[2048,256]{1,0:T(8,128)(2,1)S(1)}, u32[]{:S(2)}) %copy-start.4) | copy-done | bytes 1048600
  39.6 0.0 all-to-all-done
  39.6 0.0 copy-done.9
  39.6 1.6 %copy-done.1 = bf16[1024,1024]{1,0:T(8,128)(2,1)S(1)} copy-done((bf16[1024,1024]{1,0:T(8,128)(2,1)S(1)}, bf16[1024,1024]{1,0:T(8,128)(2,1)}, u32[]{:S(2)}) %copy-start.1) | copy-done | bytes 2097176
  41.2 1.2 %copy-done.3 = bf16[2048,256]{1,0:T(8,128)(2,1)S(1)} copy-done((bf16[2048,256]{1,0:T(8,128)(2,1)S(1)}, bf16[2048,256]{1,0:T(8,128)(2,1)}, u32[]{:S(2)}) %copy-start.3) | copy-done | bytes 1048600
  42.4 1.2 %copy-done.5 = bf16[2048,256]{1,0:T(8,128)(2,1)S(1)} copy-done((bf16[2048,256]{1,0:T(8,128)(2,1)S(1)}, bf16[2048,256]{1,0:T(8,128)(2,1)}, u32[]{:S(2)}) %copy-start.5) | copy-done | bytes 1048600
  43.6 4.7 %update.1 = f32[16,5,256]{2,1,0:T(8,128)S(1)} custom-call(s32[5,5]{1,0:T(8,128)S(1)} %copy-done.9, f32[512,128]{1,0:T(8,128)S(1)} %bitcast.9, f32[8,2048]{1,0:T(8,128)S(1)} %get-tuple-element.11.info_ref, bf16[1024,1024]{1,0:T(8,128)(2,1)S(1)} %get-tuple-element.13.pair_hi_ref, bf16[1024,1024]{1,0:T(8,128)(2,1)S(1)} %copy-done.1, ...), custom_call_target="tpu_custom_call" | custom-call | tf_op jit(solution)/shard_map/update/pallas_call | solution.py:470
  48.3 0.7 %copy.9 = f32[16,5,1,1,256]{4,3,2,1,0:T(1,128)} copy(f32[16,5,1,1,256]{4,1,0,3,2:T(8,128)S(1)} %bitcast.10) | data formatting | bytes 163840 | tf_op jit(solution)/shard_map/reshape | solution.py:479
  (10 shorter events, 0.0 us)
Async XLA Ops:
  0.0 39.6 %copy-start.9 = (s32[5,5]{1,0:T(8,128)S(1)}, s32[5,5]{1,0:T(8,128)}, u32[]{:S(2)}) copy-start(s32[5,5]{1,0:T(8,128)} %mask_ref.3) | copy-start | bytes 304
  0.0 3.9 %collective-permute-start = (f32[1,5,16,256]{3,2,1,0:T(8,128)}, f32[1,5,16,256]{3,2,1,0:T(8,128)S(1)}, u32[]{:S(2)}, u32[]{:S(2)}) collective-permute-start(f32[1,5,16,256]{3,2,1,0:T(8,128)} %own_ref.1), channel_id=1, source_target_pairs={{0,1},{1,0},{2,3},{3,2},{4,5},{5,4},{6,7},{7,6},{8,9},{9,8},{10,11... | collective-permute-start | bytes 245768 | tf_op jit(solution)/shard_map/ppermute | solution.py:424
  0.5 3.5 %collective-permute-start.1 = (f32[2,16,256]{2,1,0:T(8,128)}, f32[2,16,256]{2,1,0:T(8,128)S(1)}, u32[]{:S(2)}, u32[]{:S(2)}) collective-permute-start(f32[2,16,256]{2,1,0:T(8,128)} %vel_own_ref.1), channel_id=1, source_target_pairs={{0,1},{1,0},{2,3},{3,2},{4,5},{5,4},{6,7},{7,6},{8,9},{9,8},{10,11... | collective-permute-start | bytes 98312 | tf_op jit(solution)/shard_map/ppermute | solution.py:425
  0.6 0.7 %copy-start.10 = (s32[2048]{0:T(1024)S(1)}, s32[2048]{0:T(1024)}, u32[]{:S(2)}) copy-start(s32[2048]{0:T(1024)} %param.12) | copy-start | bytes 24580
  1.3 0.7 %copy-start.11 = (s32[2048]{0:T(1024)S(1)}, s32[2048]{0:T(1024)}, u32[]{:S(2)}) copy-start(s32[2048]{0:T(1024)} %param.11) | copy-start | bytes 24580
  2.0 0.7 %copy-start.12 = (f32[2048]{0:T(1024)S(1)}, f32[2048]{0:T(1024)}, u32[]{:S(2)}) copy-start(f32[2048]{0:T(1024)} %param.13) | copy-start | bytes 24580
  2.7 0.7 %copy-start.13 = (f32[2048]{0:T(1024)S(1)}, f32[2048]{0:T(1024)}, u32[]{:S(2)}) copy-start(f32[2048]{0:T(1024)} %param.14) | copy-start | bytes 24580
  4.0 0.9 %copy-start.6 = (f32[1,5,16,256]{3,2,1,0:T(8,128)S(1)}, f32[1,5,16,256]{3,2,1,0:T(8,128)}, u32[]{:S(2)}) copy-start(f32[1,5,16,256]{3,2,1,0:T(8,128)} %own_ref.1) | copy-start | bytes 245764
  4.8 0.8 %copy-start.7 = (f32[2,16,256]{2,1,0:T(8,128)S(1)}, f32[2,16,256]{2,1,0:T(8,128)}, u32[]{:S(2)}) copy-start(f32[2,16,256]{2,1,0:T(8,128)} %vel_own_ref.1) | copy-start | bytes 98308
  5.6 0.7 %copy-start.14 = (f32[5]{0:T(128)S(1)}, f32[5]{0:T(128)}, u32[]{:S(2)}) copy-start(f32[5]{0:T(128)} %diffusion_ref.1) | copy-start | bytes 64
  8.7 30.9 %all-to-all-start = ((f32[16,32,128]{2,1,0:T(8,128)}), f32[16,32,128]{2,1,0:T(8,128)S(1)}, u32[]{:S(2)}, u32[]{:S(2)}) async-start(f32[16,32,128]{2,1,0:T(8,128)} %bitcast.6), calls=%async_computation | async-start | bytes 524288 | tf_op jit(solution)/shard_map/all_to_all | solution.py:454
  17.0 0.7 %copy-start.8 = (s32[5,5]{1,0:T(8,128)S(1)}, s32[5,5]{1,0:T(8,128)}, u32[]{:S(2)}) copy-start(s32[5,5]{1,0:T(8,128)} %mask_ref.3) | copy-start | bytes 304
  36.3 1.3 %copy-start = (bf16[1024,1024]{1,0:T(8,128)(2,1)}, bf16[1024,1024]{1,0:T(8,128)(2,1)S(1)}, u32[]{:S(2)}) copy-start(bf16[1024,1024]{1,0:T(8,128)(2,1)S(1)} %get-tuple-element.14.pair_lo_ref) | copy-start | bytes 6291460
  37.6 1.0 %copy-start.2 = (bf16[2048,256]{1,0:T(8,128)(2,1)}, bf16[2048,256]{1,0:T(8,128)(2,1)S(1)}, u32[]{:S(2)}) copy-start(bf16[2048,256]{1,0:T(8,128)(2,1)S(1)} %get-tuple-element.15.cell_hi_ref) | copy-start | bytes 3145732
  38.6 1.0 %copy-start.4 = (bf16[2048,256]{1,0:T(8,128)(2,1)}, bf16[2048,256]{1,0:T(8,128)(2,1)S(1)}, u32[]{:S(2)}) copy-start(bf16[2048,256]{1,0:T(8,128)(2,1)S(1)} %get-tuple-element.16.cell_lo_ref) | copy-start | bytes 3145732
  39.6 1.6 %copy-start.1 = (bf16[1024,1024]{1,0:T(8,128)(2,1)S(1)}, bf16[1024,1024]{1,0:T(8,128)(2,1)}, u32[]{:S(2)}) copy-start(bf16[1024,1024]{1,0:T(8,128)(2,1)} %copy-done) | copy-start | bytes 6291460
  41.2 1.2 %copy-start.3 = (bf16[2048,256]{1,0:T(8,128)(2,1)S(1)}, bf16[2048,256]{1,0:T(8,128)(2,1)}, u32[]{:S(2)}) copy-start(bf16[2048,256]{1,0:T(8,128)(2,1)} %copy-done.2) | copy-start | bytes 3145732
  42.4 1.2 %copy-start.5 = (bf16[2048,256]{1,0:T(8,128)(2,1)S(1)}, bf16[2048,256]{1,0:T(8,128)(2,1)}, u32[]{:S(2)}) copy-start(bf16[2048,256]{1,0:T(8,128)(2,1)} %copy-done.4) | copy-start | bytes 3145732

commit v2 on v1

--- a/solution.py
+++ b/solution.py
@@ -149,12 +149,36 @@
     return n.bit_length() - 1
 
 
-def prep_kernel(order_ref, cell_ref, value_ref, var_ref, info_ref, infot_ref, *, total_rows, n_cols):
-    table_rows = cell_ref.shape[0]
-    order = order_ref[...]
+def fetch(pairs, sems):
+    copies = [pltpu.make_async_copy(src, dst, sems.at[i]) for i, (src, dst) in enumerate(pairs)]
+    for copy in copies:
+        copy.start()
+    for copy in copies:
+        copy.wait()
+
+
+def prep_kernel(
+    order_hbm, cell_hbm, value_hbm, var_hbm, mask_hbm, diffusion_hbm, stack_hbm, velocity_hbm,
+    info_ref, own_ref, vel_ref, kappa_ref,
+    order_buf, cell_buf, value_buf, var_buf, mask_buf, diffusion_buf, sems,
+    *, total_rows, n_cols,
+):
+    fetch(
+        [
+            (order_hbm, order_buf), (cell_hbm, cell_buf), (value_hbm, value_buf),
+            (var_hbm, var_buf), (mask_hbm, mask_buf), (diffusion_hbm, diffusion_buf),
+            (stack_hbm, own_ref), (velocity_hbm, vel_ref),
+        ],
+        sems,
+    )
+    table_rows = cell_buf.shape[0]
+    n_fields = mask_buf.shape[0]
+    for f in range(n_fields):
+        kappa_ref[f : f + 1, :] = jnp.full((1, LANES), diffusion_buf[0, f], jnp.float32)
+    order = order_buf[...]
     n_obs = order.shape[1]
     table = jnp.concatenate(
-        [cell_ref[...].astype(jnp.float32), value_ref[...], var_ref[...]], axis=0
+        [cell_buf[...].astype(jnp.float32), value_buf[...], var_buf[...]], axis=0
     )
     parts = jnp.concatenate(split_three(table), axis=0)
     lane_hot = (
@@ -176,16 +200,25 @@
     col = cell & (n_cols - 1)
     as_float = lambda x: x.astype(jnp.float32)
     zero = jnp.zeros((1, n_obs), jnp.float32)
+    up = lax.broadcasted_iota(jnp.int32, (8, 8), 0)
+    along = lax.broadcasted_iota(jnp.int32, (8, 8), 1)
+    mask = jnp.zeros((8, 8), jnp.float32)
+    for f in range(n_fields):
+        for b in range(n_fields):
+            mask = jnp.where((up == f) & (along == b), as_float(mask_buf[f, b]), mask)
+    field_hot = as_float(lax.broadcasted_iota(jnp.int32, (8, n_obs), 0) == field)
     info = jnp.concatenate(
-        [as_float(field), as_float(row), as_float(col), take(1), take(2), as_float(strip), zero, zero],
+        [
+            as_float(field), as_float(row), as_float(col), take(1), take(2), as_float(strip), zero, zero,
+            bdot(mask.astype(jnp.bfloat16), field_hot.astype(jnp.bfloat16)),
+        ],
         axis=0,
     )
     info_ref[...] = info
-    infot_ref[...] = info.T
 
 
 def forecast_kernel(
-    place_ref, diffusion_ref, own_ref, other_ref, vel_own_ref, vel_other_ref, info_ref,
+    place_ref, kappa_ref, own_ref, other_ref, vel_own_ref, vel_other_ref, info_ref,
     send_ref, field_buf, vel_buf, prior_buf,
 ):
     n_fields, n_rows, n_cols = field_buf.shape
@@ -206,7 +239,7 @@
     v_pos, v_neg = jnp.maximum(v, 0.0), jnp.minimum(v, 0.0)
     outflow = (u_neg - u_pos) + (v_neg - v_pos)
     for f in range(n_fields):
-        kappa = diffusion_ref[f]
+        kappa = kappa_ref[f : f + 1, 0:1]
         k_c = (1.0 - 4.0 * kappa) + outflow
         k_n = jnp.where(row == 0, 0.0, kappa + v_pos)
         k_s = jnp.where(row == n_rows - 1, 0.0, kappa - v_neg)
@@ -253,73 +286,83 @@
 
 
 def closeness_of(dist_sq):
-    inverse = lax.rsqrt(jnp.maximum(dist_sq, 1e-12))
+    inverse = lax.rsqrt(jnp.maximum(dist_sq, 1e-6))
     z = dist_sq * inverse
     half_sq = 0.5 * dist_sq
     inner = 1.0 + dist_sq * ((half_sq - 5.0 / 3.0) + z * (0.625 - 0.5 * half_sq))
-    outer = (
-        (4.0 + dist_sq * (5.0 / 3.0 - half_sq))
-        + z * (dist_sq * (dist_sq * (1.0 / 12.0) + 0.625) - 5.0)
-        - (2.0 / 3.0) * inverse
-    )
-    return jnp.where(dist_sq <= 1.0, inner, jnp.where(dist_sq <= 4.0, outer, 0.0))
+    left = jnp.maximum(2.0 - z, 0.0)
+    left = left * left
+    left = left * left
+    outer = left * ((dist_sq + (z + z)) - 0.5) * (inverse * (1.0 / 12.0))
+    return jnp.where(dist_sq <= 1.0, inner, outer)
 
 
 def loc_kernel(
-    place_ref, mask_ref, info_ref, infot_ref,
-    pair_hi_ref, pair_lo_ref, cell_hi_ref, cell_lo_ref, allow_buf,
+    place_ref, info_ref, pair_hi_hbm, pair_lo_hbm, cell_hi_ref, cell_lo_ref,
+    infot_ref, pair_hi_ref, pair_lo_ref, allow_buf, row_k_buf, col_k_buf, row_j_buf, col_j_buf, sems,
 ):
     n_obs = info_ref.shape[1]
-    batch = n_obs // BATCHES
-    n_fields = mask_ref.shape[0]
+    batch, n_pair = pair_hi_ref.shape
     n_cols = cell_hi_ref.shape[1]
     scale = 1.0 / LOC_HALF
-    step = 16
-    field_j = info_ref[0:1, batch:].astype(jnp.int32)
-    hot_j = (lax.broadcasted_iota(jnp.int32, (8, n_obs - batch), 0) == field_j).astype(jnp.float32)
-    field_k = infot_ref[0:batch, 0:1].astype(jnp.int32)
-    lane = lax.broadcasted_iota(jnp.int32, (1, 8), 1)
-    reach = jnp.zeros((batch, 8), jnp.float32)
-    for b in range(n_fields):
-        line = jnp.zeros((1, 8), jnp.float32)
-        for a in range(n_fields):
-            line = jnp.where(lane == a, mask_ref[a, b].astype(jnp.float32), line)
-        reach = jnp.where(field_k == b, line, reach)
-    allow_buf[...] = bdot(reach.astype(jnp.bfloat16), hot_j.astype(jnp.bfloat16))
-
-    half = 512
+    infot_ref[...] = info_ref[...].T
+    hot_j = (
+        lax.broadcasted_iota(jnp.int32, (8, n_pair), 0) == info_ref[0:1, batch:].astype(jnp.int32)
+    ).astype(jnp.float32)
+    allow_buf[...] = bdot(infot_ref[0:batch, 8:16].astype(jnp.bfloat16), hot_j.astype(jnp.bfloat16))
+    row_k_buf[...] = jnp.broadcast_to(infot_ref[0:batch, 1:2] * scale, (batch, LANES))
+    col_k_buf[...] = jnp.broadcast_to(infot_ref[0:batch, 2:3] * scale, (batch, LANES))
+    row_j_buf[...] = jnp.broadcast_to(info_ref[1:2, batch:] * scale, (8, n_pair))
+    col_j_buf[...] = jnp.broadcast_to(info_ref[2:3, batch:] * scale, (8, n_pair))
+    step = 128
+    tiles = (step // 8, 8, LANES)
+
+    def copies_out(i):
+        rows = pl.ds(pl.multiple_of(i * step, step), step)
+        return [
+            pltpu.make_async_copy(ref.at[rows, :], hbm.at[rows, :], sems.at[i, side])
+            for side, (ref, hbm) in enumerate([(pair_hi_ref, pair_hi_hbm), (pair_lo_ref, pair_lo_hbm)])
+        ]
 
     def pair_body(i, carry):
         at = pl.multiple_of(i * step, step)
-        row_k = infot_ref[pl.ds(at, step), 1:2] * scale
-        col_k = infot_ref[pl.ds(at, step), 2:3] * scale
-        for h in range((n_obs - batch) // half):
-            here = slice(h * half, (h + 1) * half)
-            there = slice(batch + h * half, batch + (h + 1) * half)
-            d_row = info_ref[1:2, there] * scale - row_k
-            d_col = info_ref[2:3, there] * scale - col_k
-            loc = closeness_of(d_row * d_row + d_col * d_col) * allow_buf[pl.ds(at, step), here]
-            high, low = split_two(loc)
+        row_k = row_k_buf[pl.ds(at, step), :].reshape(tiles)
+        col_k = col_k_buf[pl.ds(at, step), :].reshape(tiles)
+        for h in range(n_pair // LANES):
+            here = slice(h * LANES, (h + 1) * LANES)
+            d_row = row_j_buf[:, here][None] - row_k
+            d_col = col_j_buf[:, here][None] - col_k
+            loc = closeness_of(d_row * d_row + d_col * d_col).reshape(step, LANES)
+            high, low = split_two(loc * allow_buf[pl.ds(at, step), here])
             pair_hi_ref[pl.ds(at, step), here] = high
             pair_lo_ref[pl.ds(at, step), here] = low
+        for copy in copies_out(i):
+            copy.start()
         return carry
 
     lax.fori_loop(0, batch // step, pair_body, 0)
 
-    own_row = place_ref[1].astype(jnp.float32) * scale
-    col_j = lax.broadcasted_iota(jnp.int32, (step, n_cols), 1).astype(jnp.float32) * scale
-
-    def cell_body(i, carry):
-        for h in range(2):
-            at = pl.multiple_of(i * (2 * step) + h * step, step)
-            d_row = infot_ref[pl.ds(at, step), 1:2] * scale - own_row
-            d_col = col_j - infot_ref[pl.ds(at, step), 2:3] * scale
-            high, low = split_two(closeness_of(d_row * d_row + d_col * d_col))
-            cell_hi_ref[pl.ds(at, step), :] = high
-            cell_lo_ref[pl.ds(at, step), :] = low
-        return carry
-
-    lax.fori_loop(0, n_obs // (2 * step), cell_body, 0)
+    table_rows = 32
+    own_row = place_ref[1].astype(jnp.float32)
+    gap_row = (lax.broadcasted_iota(jnp.int32, (table_rows, LANES), 0).astype(jnp.float32) - own_row) * scale
+    gap_col = lax.broadcasted_iota(jnp.int32, (table_rows, LANES), 1).astype(jnp.float32) * scale
+    high, mid, low = split_three(closeness_of(gap_row * gap_row + gap_col * gap_col))
+    row_ids = lax.broadcasted_iota(jnp.int32, (1, table_rows), 1)
+    for b in range(BATCHES):
+        span = slice(b * batch, (b + 1) * batch)
+        hot = (row_ids == infot_ref[span, 1:2].astype(jnp.int32)).astype(jnp.float32).astype(jnp.bfloat16)
+        table = (bdot(hot, high) + bdot(hot, mid)) + bdot(hot, low)
+        col_k = jnp.broadcast_to(infot_ref[span, 2:3], (batch, LANES)).astype(jnp.int32)
+        for h in range(n_cols // LANES):
+            here = slice(h * LANES, (h + 1) * LANES)
+            col = lax.broadcasted_iota(jnp.int32, (batch, LANES), 1) + h * LANES
+            gap = jnp.minimum(jnp.abs(col - col_k), LANES - 1)
+            at_hi, at_lo = split_two(jnp.take_along_axis(table, gap, axis=1))
+            cell_hi_ref[span, here] = at_hi
+            cell_lo_ref[span, here] = at_lo
+    for i in range(batch // step):
+        for copy in copies_out(i):
+            copy.wait()
 
 
 def member_roll(x, shift):
@@ -353,12 +396,17 @@
 
 
 def update_kernel(
-    mask_ref, recv_ref, info_ref, pair_hi_ref, pair_lo_ref, cell_hi_ref, cell_lo_ref,
-    out_ref, fac_buf, *, members,
+    recv_ref, info_ref, pair_hi_hbm, pair_lo_hbm, cell_hi_ref, cell_lo_ref,
+    out_ref, fac_buf, pair_hi_ref, pair_lo_ref, sems, *, members, n_fields,
 ):
+    copies = [
+        pltpu.make_async_copy(pair_hi_hbm, pair_hi_ref, sems.at[0]),
+        pltpu.make_async_copy(pair_lo_hbm, pair_lo_ref, sems.at[1]),
+    ]
+    for copy in copies:
+        copy.start()
     n_obs = info_ref.shape[1]
     batch = n_obs // BATCHES
-    n_fields = mask_ref.shape[0]
     chunk = recv_ref.shape[0] // members
     per_chunk = n_obs // LANES
     lead = chunk - per_chunk
@@ -382,21 +430,19 @@
             high, low = split_two(r)
             fac_buf[i * members : (i + 1) * members, :] = high
             fac_buf[size + i * members : size + (i + 1) * members, :] = low
+        for f in range(n_fields):
+            masked = fac_buf[...] * info_ref[8 + f : 9 + f, span].astype(jnp.bfloat16)
+            first = bdot(masked, cell_hi_ref[span, :])
+            sums = (first[:size] + first[size:]) + bdot(masked[:size], cell_lo_ref[span, :])
+            state[f] = combined(state[f], sums)
         if b == 0:
+            for copy in copies:
+                copy.wait()
             first = bdot(fac_buf[...], pair_hi_ref[...])
             sums = (first[:size] + first[size:]) + bdot(fac_buf[:size, :], pair_lo_ref[...])
             current = combined(upcoming, sums)
-        obs_field = info_ref[0:1, span].astype(jnp.int32)
-        for f in range(n_fields):
-            open_to = jnp.zeros((1, batch), jnp.float32)
-            for a in range(n_fields):
-                open_to = jnp.where(obs_field == a, mask_ref[f, a].astype(jnp.float32), open_to)
-            masked = fac_buf[...] * open_to.astype(jnp.bfloat16)
-            first = bdot(masked, cell_hi_ref[span, :])
-            sums = (first[:size] + first[size:]) + bdot(masked[:size], cell_lo_ref[span, :])
-            state[f] = combined(state[f], sums)
     for f in range(n_fields):
-        out_ref[:, f, :] = state[f]
+        out_ref[:, f, 0, 0, :] = state[f]
 
 
 def vmem_spec():
@@ -405,6 +451,14 @@
 
 def smem_spec():
     return pl.BlockSpec(memory_space=pltpu.SMEM)
+
+
+def hbm_spec():
+    return pl.BlockSpec(memory_space=pltpu.HBM)
+
+
+def in_hbm(x):
+    return pltpu.with_memory_space_constraint(x, pltpu.HBM)
 
 
 def quick_device(
@@ -418,65 +472,96 @@
     slab_index = lax.axis_index("row")
     own_row = slab_index * rows_here + lax.axis_index("mem")
     place = jnp.stack([slab_index, own_row]).astype(jnp.int32)
-    params = pltpu.CompilerParams(vmem_limit_bytes=40 * MEGA)
+    params = pltpu.CompilerParams(vmem_limit_bytes=16 * MEGA)
     shape = jax.ShapeDtypeStruct
+    f32, i32 = jnp.float32, jnp.int32
     swap = [(0, 1), (1, 0)]
     other = lax.ppermute(realization_stack, "row", swap)
     vel_other = lax.ppermute(velocity, "row", swap)
     table = (n_obs // LANES, LANES)
-    info, infot = pl.pallas_call(
+    info, own, vel_own, kappa = pl.pallas_call(
         functools.partial(prep_kernel, total_rows=total_rows, n_cols=n_cols),
-        out_shape=(shape((8, n_obs), jnp.float32), shape((n_obs, 8), jnp.float32)),
-        in_specs=[vmem_spec()] * 4,
-        out_specs=(vmem_spec(), vmem_spec()),
+        out_shape=(
+            shape((16, n_obs), f32),
+            shape(realization_stack.shape, f32),
+            shape(velocity.shape, f32),
+            shape((8, LANES), f32),
+        ),
+        in_specs=[hbm_spec()] * 8,
+        out_specs=(vmem_spec(),) * 4,
+        scratch_shapes=[
+            pltpu.VMEM((1, n_obs), i32),
+            pltpu.VMEM(table, i32),
+            pltpu.VMEM(table, f32),
+            pltpu.VMEM(table, f32),
+            pltpu.SMEM(field_mask.shape, i32),
+            pltpu.SMEM((1, n_fields), f32),
+            pltpu.SemaphoreType.DMA((8,)),
+        ],
         compiler_params=params,
         name="prep",
     )(
-        obs_order.reshape(1, n_obs),
-        obs_cell.reshape(table),
-        obs_value.reshape(table),
-        obs_var.reshape(table),
+        in_hbm(obs_order.reshape(1, n_obs)),
+        in_hbm(obs_cell.reshape(table)),
+        in_hbm(obs_value.reshape(table)),
+        in_hbm(obs_var.reshape(table)),
+        in_hbm(field_mask),
+        in_hbm(diffusion.reshape(1, n_fields)),
+        in_hbm(realization_stack),
+        in_hbm(velocity),
     )
     chunk = -(-(n_fields * n_cols + n_obs) // (8 * LANES)) * 8
     send = pl.pallas_call(
         forecast_kernel,
-        out_shape=shape((n_mem * chunk, LANES), jnp.float32),
-        in_specs=[smem_spec(), smem_spec()] + [vmem_spec()] * 5,
+        out_shape=shape((n_mem * chunk, LANES), f32),
+        in_specs=[smem_spec()] + [vmem_spec()] * 6,
         out_specs=vmem_spec(),
         scratch_shapes=[
-            pltpu.VMEM((n_fields, total_rows, n_cols), jnp.float32),
-            pltpu.VMEM((2, total_rows, n_cols), jnp.float32),
-            pltpu.VMEM((n_obs // LANES, LANES), jnp.float32),
+            pltpu.VMEM((n_fields, total_rows, n_cols), f32),
+            pltpu.VMEM((2, total_rows, n_cols), f32),
+            pltpu.VMEM((n_obs // LANES, LANES), f32),
         ],
         compiler_params=params,
         name="forecast",
-    )(place, diffusion, realization_stack, other, velocity, vel_other, info)
+    )(place, kappa, own, other, vel_own, vel_other, info)
     recv = lax.all_to_all(send, "mem", split_axis=0, concat_axis=0, tiled=True)
-    locs = pl.pallas_call(
+    n_pair = n_obs - batch
+    pair = pltpu.HBM((batch, n_pair), jnp.bfloat16)
+    near = shape((n_obs, n_cols), jnp.bfloat16)
+    pair_hi, pair_lo, cell_hi, cell_lo = pl.pallas_call(
         loc_kernel,
-        out_shape=(
-            shape((batch, n_obs - batch), jnp.bfloat16),
-            shape((batch, n_obs - batch), jnp.bfloat16),
-            shape((n_obs, n_cols), jnp.bfloat16),
-            shape((n_obs, n_cols), jnp.bfloat16),
-        ),
-        in_specs=[smem_spec(), smem_spec(), vmem_spec(), vmem_spec()],
-        out_specs=(vmem_spec(),) * 4,
-        scratch_shapes=[pltpu.VMEM((batch, n_obs - batch), jnp.float32)],
+        out_shape=(pair, pair, near, near),
+        in_specs=[smem_spec(), vmem_spec()],
+        out_specs=(hbm_spec(), hbm_spec(), vmem_spec(), vmem_spec()),
+        scratch_shapes=[
+            pltpu.VMEM((n_obs, 16), f32),
+            pltpu.VMEM((batch, n_pair), jnp.bfloat16),
+            pltpu.VMEM((batch, n_pair), jnp.bfloat16),
+            pltpu.VMEM((batch, n_pair), f32),
+            pltpu.VMEM((batch, LANES), f32),
+            pltpu.VMEM((batch, LANES), f32),
+            pltpu.VMEM((8, n_pair), f32),
+            pltpu.VMEM((8, n_pair), f32),
+            pltpu.SemaphoreType.DMA((batch // LANES, 2)),
+        ],
         compiler_params=params,
         name="localize",
-    )(place, field_mask, info, infot)
+    )(place, info)
     rows = n_mem * (n_mem // 2 + 2)
-    out = pl.pallas_call(
-        functools.partial(update_kernel, members=n_mem),
-        out_shape=shape((n_mem, n_fields, n_cols), jnp.float32),
-        in_specs=[smem_spec()] + [vmem_spec()] * 6,
+    return pl.pallas_call(
+        functools.partial(update_kernel, members=n_mem, n_fields=n_fields),
+        out_shape=shape((n_mem, n_fields, 1, 1, n_cols), f32),
+        in_specs=[vmem_spec(), vmem_spec(), hbm_spec(), hbm_spec(), vmem_spec(), vmem_spec()],
         out_specs=vmem_spec(),
-        scratch_shapes=[pltpu.VMEM((2 * rows, batch), jnp.bfloat16)],
+        scratch_shapes=[
+            pltpu.VMEM((2 * rows, batch), jnp.bfloat16),
+            pltpu.VMEM((batch, n_pair), jnp.bfloat16),
+            pltpu.VMEM((batch, n_pair), jnp.bfloat16),
+            pltpu.SemaphoreType.DMA((2,)),
+        ],
         compiler_params=params,
         name="update",
-    )(field_mask, recv, info, *locs)
-    return out.reshape(n_mem, n_fields, 1, 1, n_cols)
+    )(recv, info, in_hbm(pair_hi), in_hbm(pair_lo), cell_hi, cell_lo)
 
 
 def is_quick(realization_stack, obs_cell, n_mem, n_slab):
@@ -487,6 +572,7 @@
         and local_members == 1
         and n_mem == rows_here == 16
         and n_fields <= 8
+        and LOC_HALF * 2 <= LANES - 1
         and powers
         and n_cols % LANES == 0
         and obs_cell.shape[0] == 8 * n_cols

time: 49.7 us -> 29.6 us (0.60)
  local copies, waits for them, and re-layouts: 13.8 us -> 0 us
  Pallas kernels: 26.2 us -> 19.4 us
  waiting for transfers between devices: 0.01 us -> 1.01 us
    unnamed x30 -> x0, local copies, waits for them, and re-layouts: 13.1 us -> none
    pallas_call x3, Pallas kernels: 25.7 us -> 17.9 us  [the longest x1 9.03 us: quick_device(): pl.pallas_call(loc_kernel, out_shape=(pair, pair, near, near), in_specs=[...]
    all_to_all x1, waiting for transfers between devices: 0.01 us -> 1 us  [quick_device(): recv = lax.all_to_all(send, 'mem', split_axis=0, concat_axis=0, tiled=True)]
    pallas_call x1, Pallas kernels: 0.54 us -> 1.46 us  [quick_device(): pl.pallas_call(functools.partial(prep_kernel, total_rows=total_rows, n_co...]
    reshape x1 -> x0, local copies, waits for them, and re-layouts: 0.72 us -> none  [quick_device(): return out.reshape(n_mem, n_fields, 1, 1, n_cols)]
  transfers between devices with their start and end apart: 3 -> 3, of which waited for: 0 -> 1; matrix products, arithmetic and copies ran while one was open for 0% -> 0% of each run, Pallas kernels for 39% -> 36%
where the time goes in v2:
time: 29.6 us; the launch traced here: 29.3 us
  Pallas kernels  19.4 us (66%)
  starting transfers between devices  8.82 us (30%)
  waiting for transfers between devices  1.01 us (3%)
    pallas_call x1, Pallas kernels, quick_device(): pl.pallas_call(loc_kernel, out_shape=(pair, pair, near, near), in_specs=[...  9.03 us
    all_to_all x1, starting transfers between devices, quick_device(): recv = lax.all_to_all(send, 'mem', split_axis=0, concat_axis=0, tiled=True)  8.31 us
    pallas_call x1, Pallas kernels, quick_device(): pl.pallas_call(functools.partial(update_kernel, members=n_mem, n_fields=n...  6.45 us
    pallas_call x1, Pallas kernels, quick_device(): pl.pallas_call(forecast_kernel, out_shape=shape((n_mem * chunk, LANES), f...  2.43 us
    pallas_call x1, Pallas kernels, quick_device(): pl.pallas_call(functools.partial(prep_kernel, total_rows=total_rows, n_co...  1.46 us
    all_to_all x1, waiting for transfers between devices, quick_device(): recv = lax.all_to_all(send, 'mem', split_axis=0, concat_axis=0, tiled=True)  1 us
  transfers between devices with their start and end apart: 3, of which 1 were waited for; matrix products, arithmetic and copies ran while one was open for 0% of the time, Pallas kernels for 36%

profile of v2, /device:TPU:0, one launch (start us, length us, event | category | flops | bytes accessed | tf_op | source)
XLA Modules:
  0.0 29.3 jit_solution(8764434474030633792)
XLA Ops:
  0.0 0.5 %collective-permute-start.1 = (f32[2,16,256]{2,1,0:T(8,128)}, f32[2,16,256]{2,1,0:T(8,128)S(1)}, u32[]{:S(2)}, u32[]{:S(2)}) collective-permute-start(f32[2,16,256]{2,1,0:T(8,128)} %velocity_hbm.1), channel_id=1, source_target_pairs={{0,1},{1,0},{2,3},{3,2},{4,5},{5,4},{6,7},{7,6},{8,9},{9,8},{10,11... | collective-permute-start | bytes 98312 | tf_op jit(solution)/shard_map/ppermute | solution.py:480
  0.5 0.1 collective-permute-start
  0.5 0.1 pad_add_fusion.place_ref
  0.6 1.5 %prep.1 = (f32[16,2048]{1,0:T(8,128)S(1)}, f32[1,5,16,256]{3,2,1,0:T(8,128)S(1)}, f32[2,16,256]{2,1,0:T(8,128)S(1)}, f32[8,128]{1,0:T(8,128)S(1)}) custom-call(s32[1,2048]{1,0:T(1,128)} %bitcast.10, s32[16,128]{1,0:T(8,128)} %bitcast.11, f32[16,128]{1,0:T(8,128)} %bitcast.12, f32[16,128]{1,0:T(8,128)} %bitcast.13, s32[5,5]{1,0:T(8,128)} %mask_hbm.1, ...), custom_call_target="tpu_custom_call" | custom-call | tf_op jit(solution)/shard_map/prep/pallas_call | solution.py:482
  2.1 0.0 collective-permute-done.1.vel_other_ref
  2.1 0.0 collective-permute-done.other_ref
  2.1 2.4 %forecast.1 = f32[512,128]{1,0:T(8,128)} custom-call(s32[2]{0:T(128)S(1)} %pad_add_fusion.place_ref, f32[8,128]{1,0:T(8,128)S(1)} %get-tuple-element.13.kappa_ref, f32[1,5,16,256]{3,2,1,0:T(8,128)S(1)} %get-tuple-element.14.own_ref, f32[1,5,16,256]{3,2,1,0:T(8,128)S(1)} %collective-permute-done.other_ref, f32[2,16,256]{2,1,0:T(8,128)S(1)} %get-tuple-element.15.vel_own_ref, ...), custom_call_target="tpu_custom_call" | custom-call | tf_op jit(solution)/shard_map/forecast/pallas_call | solution.py:514
  4.5 8.3 %all-to-all-start = ((f32[16,32,128]{2,1,0:T(8,128)}), f32[16,32,128]{2,1,0:T(8,128)S(1)}, u32[]{:S(2)}, u32[]{:S(2)}) async-start(f32[16,32,128]{2,1,0:T(8,128)} %bitcast.7), calls=%async_computation | async-start | bytes 524288 | tf_op jit(solution)/shard_map/all_to_all | solution.py:527
  12.8 9.0 %localize.1 = (bf16[1024,1024]{1,0:T(8,128)(2,1)}, bf16[1024,1024]{1,0:T(8,128)(2,1)}, bf16[2048,256]{1,0:T(8,128)(2,1)S(1)}, bf16[2048,256]{1,0:T(8,128)(2,1)S(1)}) custom-call(s32[2]{0:T(128)S(1)} %pad_add_fusion.place_ref, f32[16,2048]{1,0:T(8,128)S(1)} %get-tuple-element.16.info_ref), custom_call_target="tpu_custom_call" | custom-call | tf_op jit(solution)/shard_map/localize/pallas_call | solution.py:531
  21.9 1.0 %all-to-all-done = f32[16,32,128]{2,1,0:T(8,128)S(1)} async-done(((f32[16,32,128]{2,1,0:T(8,128)}), f32[16,32,128]{2,1,0:T(8,128)S(1)}, u32[]{:S(2)}, u32[]{:S(2)}) %all-to-all-start) | async-done | bytes 262176 | tf_op jit(solution)/shard_map/all_to_all | solution.py:527
  22.9 6.5 %update.1 = f32[16,5,1,1,256]{4,3,2,1,0:T(1,128)} custom-call(f32[512,128]{1,0:T(8,128)S(1)} %bitcast.9, f32[16,2048]{1,0:T(8,128)S(1)} %get-tuple-element.16.info_ref, bf16[1024,1024]{1,0:T(8,128)(2,1)} %get-tuple-element.17.pair_hi_hbm, bf16[1024,1024]{1,0:T(8,128)(2,1)} %get-tuple-element.18.pair_lo_hbm, ...), custom_call_target="tpu_custom_call" | custom-call | tf_op jit(solution)/shard_map/update/pallas_call | solution.py:551
Async XLA Ops:
  0.0 2.1 %collective-permute-start.1 = (f32[2,16,256]{2,1,0:T(8,128)}, f32[2,16,256]{2,1,0:T(8,128)S(1)}, u32[]{:S(2)}, u32[]{:S(2)}) collective-permute-start(f32[2,16,256]{2,1,0:T(8,128)} %velocity_hbm.1), channel_id=1, source_target_pairs={{0,1},{1,0},{2,3},{3,2},{4,5},{5,4},{6,7},{7,6},{8,9},{9,8},{10,11... | collective-permute-start | bytes 98312 | tf_op jit(solution)/shard_map/ppermute | solution.py:480
  0.5 1.6 %collective-permute-start = (f32[1,5,16,256]{3,2,1,0:T(8,128)}, f32[1,5,16,256]{3,2,1,0:T(8,128)S(1)}, u32[]{:S(2)}, u32[]{:S(2)}) collective-permute-start(f32[1,5,16,256]{3,2,1,0:T(8,128)} %stack_hbm.1), channel_id=1, source_target_pairs={{0,1},{1,0},{2,3},{3,2},{4,5},{5,4},{6,7},{7,6},{8,9},{9,8},{10,11... | collective-permute-start | bytes 245768 | tf_op jit(solution)/shard_map/ppermute | solution.py:479
  4.5 18.4 %all-to-all-start = ((f32[16,32,128]{2,1,0:T(8,128)}), f32[16,32,128]{2,1,0:T(8,128)S(1)}, u32[]{:S(2)}, u32[]{:S(2)}) async-start(f32[16,32,128]{2,1,0:T(8,128)} %bitcast.7), calls=%async_computation | async-start | bytes 524288 | tf_op jit(solution)/shard_map/all_to_all | solution.py:527

commit v3 on v2

--- a/solution.py
+++ b/solution.py
@@ -149,10 +149,14 @@
     return n.bit_length() - 1
 
 
-def fetch(pairs, sems):
+def start_copies(pairs, sems):
     copies = [pltpu.make_async_copy(src, dst, sems.at[i]) for i, (src, dst) in enumerate(pairs)]
     for copy in copies:
         copy.start()
+    return copies
+
+
+def finish(copies):
     for copy in copies:
         copy.wait()
 
@@ -163,18 +167,17 @@
     order_buf, cell_buf, value_buf, var_buf, mask_buf, diffusion_buf, sems,
     *, total_rows, n_cols,
 ):
-    fetch(
+    copies = start_copies(
         [
-            (order_hbm, order_buf), (cell_hbm, cell_buf), (value_hbm, value_buf),
-            (var_hbm, var_buf), (mask_hbm, mask_buf), (diffusion_hbm, diffusion_buf),
-            (stack_hbm, own_ref), (velocity_hbm, vel_ref),
+            (order_hbm, order_buf), (cell_hbm, cell_buf), (value_hbm, value_buf), (var_hbm, var_buf),
+            (mask_hbm, mask_buf), (diffusion_hbm, diffusion_buf), (velocity_hbm, vel_ref),
+            (stack_hbm, own_ref),
         ],
         sems,
     )
+    finish(copies[:4])
     table_rows = cell_buf.shape[0]
     n_fields = mask_buf.shape[0]
-    for f in range(n_fields):
-        kappa_ref[f : f + 1, :] = jnp.full((1, LANES), diffusion_buf[0, f], jnp.float32)
     order = order_buf[...]
     n_obs = order.shape[1]
     table = jnp.concatenate(
@@ -200,6 +203,9 @@
     col = cell & (n_cols - 1)
     as_float = lambda x: x.astype(jnp.float32)
     zero = jnp.zeros((1, n_obs), jnp.float32)
+    finish(copies[4:])
+    for f in range(n_fields):
+        kappa_ref[f : f + 1, :] = jnp.full((1, LANES), diffusion_buf[0, f], jnp.float32)
     up = lax.broadcasted_iota(jnp.int32, (8, 8), 0)
     along = lax.broadcasted_iota(jnp.int32, (8, 8), 1)
     mask = jnp.zeros((8, 8), jnp.float32)
@@ -219,20 +225,19 @@
 
 def forecast_kernel(
     place_ref, kappa_ref, own_ref, other_ref, vel_own_ref, vel_other_ref, info_ref,
-    send_ref, field_buf, vel_buf, prior_buf,
+    send_ref, field_buf, prior_buf,
 ):
     n_fields, n_rows, n_cols = field_buf.shape
     half = n_rows // 2
     n_dest = half
     chunk = send_ref.shape[0] // n_dest
-    mine = pl.multiple_of(place_ref[0] * half, half)
-    theirs = pl.multiple_of((1 - place_ref[0]) * half, half)
-    vel_buf[:, pl.ds(mine, half), :] = vel_own_ref[...]
-    vel_buf[:, pl.ds(theirs, half), :] = vel_other_ref[...]
-    field_buf[:, pl.ds(mine, half), :] = own_ref[0]
-    field_buf[:, pl.ds(theirs, half), :] = other_ref[0]
-    u = vel_buf[0]
-    v = vel_buf[1]
+    first_slab = place_ref[0:1, 0:1] < 0.5
+
+    def whole_of(own, other):
+        return jnp.concatenate([jnp.where(first_slab, own, other), jnp.where(first_slab, other, own)], axis=0)
+
+    u = whole_of(vel_own_ref[0], vel_other_ref[0])
+    v = whole_of(vel_own_ref[1], vel_other_ref[1])
     row = lax.broadcasted_iota(jnp.int32, (n_rows, n_cols), 0)
     col = lax.broadcasted_iota(jnp.int32, (n_rows, n_cols), 1)
     u_pos, u_neg = jnp.maximum(u, 0.0), jnp.minimum(u, 0.0)
@@ -245,7 +250,7 @@
         k_s = jnp.where(row == n_rows - 1, 0.0, kappa - v_neg)
         k_w = jnp.where(col == 0, 0.0, kappa + u_pos)
         k_e = jnp.where(col == n_cols - 1, 0.0, kappa - u_neg)
-        c = field_buf[f]
+        c = whole_of(own_ref[0, f], other_ref[0, f])
         for _ in range(SUBSTEPS):
             c = (
                 (c * k_c + pltpu.roll(c, 1, 0) * k_n)
@@ -276,7 +281,7 @@
         send_ref[d * chunk + lead : (d + 1) * chunk, :] = priors
     pieces = n_cols // LANES
     for f in range(n_fields):
-        rows = field_buf[f, pl.ds(mine, half), :]
+        rows = jnp.where(first_slab, field_buf[f, :half, :], field_buf[f, half:, :])
         for h in range(pieces):
             send_ref[pl.ds(f * pieces + h, n_dest, stride=chunk), :] = rows[
                 :, h * LANES : (h + 1) * LANES
@@ -298,61 +303,45 @@
 
 
 def loc_kernel(
-    place_ref, info_ref, pair_hi_hbm, pair_lo_hbm, cell_hi_ref, cell_lo_ref,
-    infot_ref, pair_hi_ref, pair_lo_ref, allow_buf, row_k_buf, col_k_buf, row_j_buf, col_j_buf, sems,
+    place_ref, info_ref, pair_hi_ref, pair_lo_ref, rest_hbm, cell_hi_hbm, cell_lo_hbm,
+    infot_ref, rest_ref, cell_hi_ref, cell_lo_ref, gap_buf, sems,
 ):
     n_obs = info_ref.shape[1]
     batch, n_pair = pair_hi_ref.shape
     n_cols = cell_hi_ref.shape[1]
     scale = 1.0 / LOC_HALF
-    infot_ref[...] = info_ref[...].T
-    hot_j = (
-        lax.broadcasted_iota(jnp.int32, (8, n_pair), 0) == info_ref[0:1, batch:].astype(jnp.int32)
-    ).astype(jnp.float32)
-    allow_buf[...] = bdot(infot_ref[0:batch, 8:16].astype(jnp.bfloat16), hot_j.astype(jnp.bfloat16))
-    row_k_buf[...] = jnp.broadcast_to(infot_ref[0:batch, 1:2] * scale, (batch, LANES))
-    col_k_buf[...] = jnp.broadcast_to(infot_ref[0:batch, 2:3] * scale, (batch, LANES))
-    row_j_buf[...] = jnp.broadcast_to(info_ref[1:2, batch:] * scale, (8, n_pair))
-    col_j_buf[...] = jnp.broadcast_to(info_ref[2:3, batch:] * scale, (8, n_pair))
-    step = 128
-    tiles = (step // 8, 8, LANES)
-
-    def copies_out(i):
-        rows = pl.ds(pl.multiple_of(i * step, step), step)
-        return [
-            pltpu.make_async_copy(ref.at[rows, :], hbm.at[rows, :], sems.at[i, side])
-            for side, (ref, hbm) in enumerate([(pair_hi_ref, pair_hi_hbm), (pair_lo_ref, pair_lo_hbm)])
-        ]
-
-    def pair_body(i, carry):
-        at = pl.multiple_of(i * step, step)
-        row_k = row_k_buf[pl.ds(at, step), :].reshape(tiles)
-        col_k = col_k_buf[pl.ds(at, step), :].reshape(tiles)
-        for h in range(n_pair // LANES):
-            here = slice(h * LANES, (h + 1) * LANES)
-            d_row = row_j_buf[:, here][None] - row_k
-            d_col = col_j_buf[:, here][None] - col_k
-            loc = closeness_of(d_row * d_row + d_col * d_col).reshape(step, LANES)
-            high, low = split_two(loc * allow_buf[pl.ds(at, step), here])
-            pair_hi_ref[pl.ds(at, step), here] = high
-            pair_lo_ref[pl.ds(at, step), here] = low
-        for copy in copies_out(i):
-            copy.start()
-        return carry
-
-    lax.fori_loop(0, batch // step, pair_body, 0)
-
+    far = 32.0 * LOC_HALF * LOC_HALF
+    row, col = info_ref[1:2, :], info_ref[2:3, :]
+    norm = [part.astype(jnp.float32) for part in split_three(row * row + col * col)]
+    one = jnp.ones((1, n_obs), jnp.float32)
+    hot = lax.broadcasted_iota(jnp.int32, (8, n_obs), 0) == info_ref[0:1, :].astype(jnp.int32)
+    zeros = jnp.zeros((6, n_obs), jnp.float32)
+    feature_k = jnp.concatenate(
+        norm + [one, one, one, -2.0 * row, -2.0 * col, -far * info_ref[8:16, :], one * far, row, zeros], axis=0
+    )
+    feature_j = jnp.concatenate(
+        [one, one, one] + norm + [row, col, hot.astype(jnp.float32), one], axis=0
+    )[:, batch:]
+    infot_ref[...] = feature_k.T
+    terms = feature_j.shape[0]
+    gap_buf[...] = bdot(
+        infot_ref[0:batch, 0:terms].astype(jnp.bfloat16), (feature_j * (scale * scale)).astype(jnp.bfloat16)
+    )
     table_rows = 32
-    own_row = place_ref[1].astype(jnp.float32)
+    own_row = place_ref[1:2, 0:1]
     gap_row = (lax.broadcasted_iota(jnp.int32, (table_rows, LANES), 0).astype(jnp.float32) - own_row) * scale
     gap_col = lax.broadcasted_iota(jnp.int32, (table_rows, LANES), 1).astype(jnp.float32) * scale
     high, mid, low = split_three(closeness_of(gap_row * gap_row + gap_col * gap_col))
     row_ids = lax.broadcasted_iota(jnp.int32, (1, table_rows), 1)
+    copies = []
+    col_at, row_at = 7, terms
     for b in range(BATCHES):
         span = slice(b * batch, (b + 1) * batch)
-        hot = (row_ids == infot_ref[span, 1:2].astype(jnp.int32)).astype(jnp.float32).astype(jnp.bfloat16)
+        rows = infot_ref[span, row_at : row_at + 1].astype(jnp.int32)
+        hot = (row_ids == rows).astype(jnp.float32).astype(jnp.bfloat16)
         table = (bdot(hot, high) + bdot(hot, mid)) + bdot(hot, low)
-        col_k = jnp.broadcast_to(infot_ref[span, 2:3], (batch, LANES)).astype(jnp.int32)
+        cols = infot_ref[span, col_at : col_at + 1] * -0.5
+        col_k = jnp.broadcast_to(cols, (batch, LANES)).astype(jnp.int32)
         for h in range(n_cols // LANES):
             here = slice(h * LANES, (h + 1) * LANES)
             col = lax.broadcasted_iota(jnp.int32, (batch, LANES), 1) + h * LANES
@@ -360,9 +349,33 @@
             at_hi, at_lo = split_two(jnp.take_along_axis(table, gap, axis=1))
             cell_hi_ref[span, here] = at_hi
             cell_lo_ref[span, here] = at_lo
-    for i in range(batch // step):
-        for copy in copies_out(i):
-            copy.wait()
+        copies += start_copies(
+            [
+                (cell_hi_ref.at[span, :], cell_hi_hbm.at[span, :]),
+                (cell_lo_ref.at[span, :], cell_lo_hbm.at[span, :]),
+            ],
+            sems.at[2 * b :],
+        )
+    step = 128
+    kept = pair_lo_ref.shape[0]
+
+    def pair_rows(low_ref, first):
+        def body(i, carry):
+            to = pl.multiple_of(i * step, step)
+            at = pl.multiple_of(first + i * step, step)
+            for h in range(n_pair // LANES):
+                here = slice(h * LANES, (h + 1) * LANES)
+                high, low = split_two(closeness_of(gap_buf[pl.ds(at, step), here]))
+                pair_hi_ref[pl.ds(at, step), here] = high
+                low_ref[pl.ds(to, step), here] = low
+            return carry
+
+        lax.fori_loop(0, low_ref.shape[0] // step, body, 0)
+
+    pair_rows(rest_ref, kept)
+    copies += start_copies([(rest_ref, rest_hbm)], sems.at[2 * BATCHES :])
+    pair_rows(pair_lo_ref, 0)
+    finish(copies)
 
 
 def member_roll(x, shift):
@@ -396,53 +409,68 @@
 
 
 def update_kernel(
-    recv_ref, info_ref, pair_hi_hbm, pair_lo_hbm, cell_hi_ref, cell_lo_ref,
-    out_ref, fac_buf, pair_hi_ref, pair_lo_ref, sems, *, members, n_fields,
+    recv_ref, info_ref, pair_hi_ref, pair_lo_ref, rest_hbm, cell_hi_hbm, cell_lo_hbm,
+    out_ref, fac_buf, sums_buf, mask_buf, rest_ref, cell_hi_ref, cell_lo_ref, sems, *, members, n_fields,
 ):
-    copies = [
-        pltpu.make_async_copy(pair_hi_hbm, pair_hi_ref, sems.at[0]),
-        pltpu.make_async_copy(pair_lo_hbm, pair_lo_ref, sems.at[1]),
-    ]
-    for copy in copies:
-        copy.start()
+    tables = [(rest_hbm, rest_ref), (cell_hi_hbm, cell_hi_ref), (cell_lo_hbm, cell_lo_ref)]
+    copies = [pltpu.make_async_copy(src, dst, sems.at[i]) for i, (src, dst) in enumerate(tables)]
     n_obs = info_ref.shape[1]
     batch = n_obs // BATCHES
     chunk = recv_ref.shape[0] // members
     per_chunk = n_obs // LANES
     lead = chunk - per_chunk
     pieces = cell_hi_ref.shape[1] // LANES
-    size = fac_buf.shape[0] // 2
+    size = fac_buf.shape[1] // 2
+    kept = pair_lo_ref.shape[0]
 
     def member_row(i):
         return recv_ref[pl.ds(i, members, stride=chunk), :]
 
-    state = [
-        jnp.concatenate([member_row(f * pieces + h) for h in range(pieces)], axis=1)
-        for f in range(n_fields)
-    ]
-    priors = jnp.concatenate([member_row(lead + q) for q in range(per_chunk)], axis=1)
-    upcoming = priors[:, batch:]
-    current = priors[:, :batch]
-    for b in range(BATCHES):
+    def priors_of(b):
+        first = lead + b * (per_chunk // BATCHES)
+        return jnp.concatenate([member_row(first + q) for q in range(per_chunk // BATCHES)], axis=1)
+
+    def set_factors(b, priors):
         span = slice(b * batch, (b + 1) * batch)
-        rows = factors(current, info_ref[3:4, span], info_ref[4:5, span])
+        rows = factors(priors, info_ref[3:4, span], info_ref[4:5, span])
         for i, r in enumerate(rows):
             high, low = split_two(r)
-            fac_buf[i * members : (i + 1) * members, :] = high
-            fac_buf[size + i * members : size + (i + 1) * members, :] = low
+            fac_buf[b, i * members : (i + 1) * members, :] = high
+            fac_buf[b, size + i * members : size + (i + 1) * members, :] = low
+
+    @pl.when(pl.program_id(0) == 0)
+    def _():
+        for copy in copies:
+            copy.start()
+        set_factors(0, priors_of(0))
+        first = bdot(fac_buf[0], pair_hi_ref[...])
+        sums_buf[...] = (first[:size] + first[size:]) + bdot(fac_buf[0, :size, :kept], pair_lo_ref[...])
+
+    @pl.when(pl.program_id(0) == 1)
+    def _():
+        finish(copies[:1])
+        sums = sums_buf[...] + bdot(fac_buf[0, :size, kept:], rest_ref[...])
+        set_factors(1, combined(priors_of(1), sums))
+
+    @pl.when(pl.program_id(0) == 2)
+    def _():
+        finish(copies[1:])
+        states = [
+            jnp.concatenate([member_row(f * pieces + h) for h in range(pieces)], axis=1)
+            for f in range(n_fields)
+        ]
+        all_rows = n_fields * size
+        for b in range(BATCHES):
+            span = slice(b * batch, (b + 1) * batch)
+            for f in range(n_fields):
+                open_to = info_ref[8 + f : 9 + f, span].astype(jnp.bfloat16)
+                mask_buf[f * size : (f + 1) * size, :] = fac_buf[b, :size, :] * open_to
+                mask_buf[all_rows + f * size : all_rows + (f + 1) * size, :] = fac_buf[b, size:, :] * open_to
+            first = bdot(mask_buf[...], cell_hi_ref[span, :])
+            sums = (first[:all_rows] + first[all_rows:]) + bdot(mask_buf[:all_rows, :], cell_lo_ref[span, :])
+            states = [combined(state, sums[f * size : (f + 1) * size]) for f, state in enumerate(states)]
         for f in range(n_fields):
-            masked = fac_buf[...] * info_ref[8 + f : 9 + f, span].astype(jnp.bfloat16)
-            first = bdot(masked, cell_hi_ref[span, :])
-            sums = (first[:size] + first[size:]) + bdot(masked[:size], cell_lo_ref[span, :])
-            state[f] = combined(state[f], sums)
-        if b == 0:
-            for copy in copies:
-                copy.wait()
-            first = bdot(fac_buf[...], pair_hi_ref[...])
-            sums = (first[:size] + first[size:]) + bdot(fac_buf[:size, :], pair_lo_ref[...])
-            current = combined(upcoming, sums)
-    for f in range(n_fields):
-        out_ref[:, f, 0, 0, :] = state[f]
+            out_ref[:, f, 0, 0, :] = states[f]
 
 
 def vmem_spec():
@@ -471,7 +499,9 @@
     batch = n_obs // BATCHES
     slab_index = lax.axis_index("row")
     own_row = slab_index * rows_here + lax.axis_index("mem")
-    place = jnp.stack([slab_index, own_row]).astype(jnp.int32)
+    place = jnp.where(
+        lax.broadcasted_iota(jnp.int32, (8, LANES), 0) == 0, slab_index, own_row
+    ).astype(jnp.float32)
     params = pltpu.CompilerParams(vmem_limit_bytes=16 * MEGA)
     shape = jax.ShapeDtypeStruct
     f32, i32 = jnp.float32, jnp.int32
@@ -510,39 +540,43 @@
         in_hbm(realization_stack),
         in_hbm(velocity),
     )
-    chunk = -(-(n_fields * n_cols + n_obs) // (8 * LANES)) * 8
+    chunk = (n_fields * n_cols + n_obs) // LANES
     send = pl.pallas_call(
         forecast_kernel,
         out_shape=shape((n_mem * chunk, LANES), f32),
-        in_specs=[smem_spec()] + [vmem_spec()] * 6,
+        in_specs=[vmem_spec()] * 7,
         out_specs=vmem_spec(),
         scratch_shapes=[
             pltpu.VMEM((n_fields, total_rows, n_cols), f32),
-            pltpu.VMEM((2, total_rows, n_cols), f32),
             pltpu.VMEM((n_obs // LANES, LANES), f32),
         ],
         compiler_params=params,
         name="forecast",
     )(place, kappa, own, other, vel_own, vel_other, info)
-    recv = lax.all_to_all(send, "mem", split_axis=0, concat_axis=0, tiled=True)
+    recv = lax.all_to_all(
+        send.reshape(n_mem, chunk, 1, LANES), "mem", split_axis=0, concat_axis=0, tiled=True
+    ).reshape(send.shape)
     n_pair = n_obs - batch
-    pair = pltpu.HBM((batch, n_pair), jnp.bfloat16)
-    near = shape((n_obs, n_cols), jnp.bfloat16)
-    pair_hi, pair_lo, cell_hi, cell_lo = pl.pallas_call(
+    bf16 = jnp.bfloat16
+    kept = batch // 2
+    pair_hi, pair_lo, rest, cell_hi, cell_lo = pl.pallas_call(
         loc_kernel,
-        out_shape=(pair, pair, near, near),
-        in_specs=[smem_spec(), vmem_spec()],
-        out_specs=(hbm_spec(), hbm_spec(), vmem_spec(), vmem_spec()),
+        out_shape=(
+            shape((batch, n_pair), bf16),
+            shape((kept, n_pair), bf16),
+            pltpu.HBM((batch - kept, n_pair), bf16),
+            pltpu.HBM((n_obs, n_cols), bf16),
+            pltpu.HBM((n_obs, n_cols), bf16),
+        ),
+        in_specs=[vmem_spec(), vmem_spec()],
+        out_specs=(vmem_spec(), vmem_spec(), hbm_spec(), hbm_spec(), hbm_spec()),
         scratch_shapes=[
-            pltpu.VMEM((n_obs, 16), f32),
-            pltpu.VMEM((batch, n_pair), jnp.bfloat16),
-            pltpu.VMEM((batch, n_pair), jnp.bfloat16),
+            pltpu.VMEM((n_obs, 24), f32),
+            pltpu.VMEM((batch - kept, n_pair), bf16),
+            pltpu.VMEM((n_obs, n_cols), bf16),
+            pltpu.VMEM((n_obs, n_cols), bf16),
             pltpu.VMEM((batch, n_pair), f32),
-            pltpu.VMEM((batch, LANES), f32),
-            pltpu.VMEM((batch, LANES), f32),
-            pltpu.VMEM((8, n_pair), f32),
-            pltpu.VMEM((8, n_pair), f32),
-            pltpu.SemaphoreType.DMA((batch // LANES, 2)),
+            pltpu.SemaphoreType.DMA((2 * BATCHES + 1,)),
         ],
         compiler_params=params,
         name="localize",
@@ -550,18 +584,22 @@
     rows = n_mem * (n_mem // 2 + 2)
     return pl.pallas_call(
         functools.partial(update_kernel, members=n_mem, n_fields=n_fields),
+        grid=(3,),
         out_shape=shape((n_mem, n_fields, 1, 1, n_cols), f32),
-        in_specs=[vmem_spec(), vmem_spec(), hbm_spec(), hbm_spec(), vmem_spec(), vmem_spec()],
+        in_specs=[vmem_spec()] * 4 + [hbm_spec()] * 3,
         out_specs=vmem_spec(),
         scratch_shapes=[
-            pltpu.VMEM((2 * rows, batch), jnp.bfloat16),
-            pltpu.VMEM((batch, n_pair), jnp.bfloat16),
-            pltpu.VMEM((batch, n_pair), jnp.bfloat16),
-            pltpu.SemaphoreType.DMA((2,)),
+            pltpu.VMEM((BATCHES, 2 * rows, batch), bf16),
+            pltpu.VMEM((rows, n_pair), f32),
+            pltpu.VMEM((2 * rows * n_fields, batch), bf16),
+            pltpu.VMEM((batch - kept, n_pair), bf16),
+            pltpu.VMEM((n_obs, n_cols), bf16),
+            pltpu.VMEM((n_obs, n_cols), bf16),
+            pltpu.SemaphoreType.DMA((3,)),
         ],
         compiler_params=params,
         name="update",
-    )(recv, info, in_hbm(pair_hi), in_hbm(pair_lo), cell_hi, cell_lo)
+    )(recv, info, pair_hi, pair_lo, in_hbm(rest), in_hbm(cell_hi), in_hbm(cell_lo))
 
 
 def is_quick(realization_stack, obs_cell, n_mem, n_slab):

time: 29.6 us -> 27.1 us (0.916)
  Pallas kernels: 19.4 us -> 15.2 us
  waiting for transfers between devices: 1.01 us -> 2.65 us
    pallas_call x1, Pallas kernels: 9.03 us -> 6.55 us  [quick_device(): pl.pallas_call(loc_kernel, out_shape=(shape((batch, n_pair), bf16), shape...]
    all_to_all x1, waiting for transfers between devices: 1 us -> 2.62 us  [quick_device(): lax.all_to_all(send.reshape(n_mem, chunk, 1, LANES), 'mem', split_axis=0,...]
    pallas_call x1, Pallas kernels: 6.45 us -> 5.44 us  [quick_device(): pl.pallas_call(functools.partial(update_kernel, members=n_mem, n_fields=n...]
    pallas_call x1, Pallas kernels: 2.43 us -> 1.83 us  [quick_device(): pl.pallas_call(forecast_kernel, out_shape=shape((n_mem * chunk, LANES), f...]
  transfers between devices with their start and end apart: 3 -> 3, of which waited for: 1 -> 1; matrix products, arithmetic and copies ran while one was open for 0% -> 0% of each run, Pallas kernels for 36% -> 30%
where the time goes in v3:
time: 27.1 us; the launch traced here: 26.8 us
  Pallas kernels  15.2 us (56%)
  starting transfers between devices  8.81 us (33%)
  waiting for transfers between devices  2.65 us (10%)
    all_to_all x1, starting transfers between devices, quick_device(): lax.all_to_all(send.reshape(n_mem, chunk, 1, LANES), 'mem', split_axis=0,...  8.3 us
    pallas_call x1, Pallas kernels, quick_device(): pl.pallas_call(loc_kernel, out_shape=(shape((batch, n_pair), bf16), shape...  6.55 us
    pallas_call x1, Pallas kernels, quick_device(): pl.pallas_call(functools.partial(update_kernel, members=n_mem, n_fields=n...  5.44 us
    all_to_all x1, waiting for transfers between devices, quick_device(): lax.all_to_all(send.reshape(n_mem, chunk, 1, LANES), 'mem', split_axis=0,...  2.62 us
    pallas_call x1, Pallas kernels, quick_device(): pl.pallas_call(forecast_kernel, out_shape=shape((n_mem * chunk, LANES), f...  1.83 us
    pallas_call x1, Pallas kernels, quick_device(): pl.pallas_call(functools.partial(prep_kernel, total_rows=total_rows, n_co...  1.38 us
  transfers between devices with their start and end apart: 3, of which 1 were waited for; matrix products, arithmetic and copies ran while one was open for 0% of the time, Pallas kernels for 30%

profile of v3, /device:TPU:0, one launch (start us, length us, event | category | flops | bytes accessed | tf_op | source)
XLA Modules:
  0.0 26.8 jit_solution(7145446723208501604)
XLA Ops:
  0.0 0.5 %collective-permute-start.1 = (f32[2,16,256]{2,1,0:T(8,128)}, f32[2,16,256]{2,1,0:T(8,128)S(1)}, u32[]{:S(2)}, u32[]{:S(2)}) collective-permute-start(f32[2,16,256]{2,1,0:T(8,128)} %velocity_hbm.1), channel_id=1, source_target_pairs={{0,1},{1,0},{2,3},{3,2},{4,5},{5,4},{6,7},{7,6},{8,9},{9,8},{10,11... | collective-permute-start | bytes 98312 | tf_op jit(solution)/shard_map/ppermute | solution.py:510
  0.5 0.1 collective-permute-start
  0.5 1.4 %prep.1 = (f32[16,2048]{1,0:T(8,128)S(1)}, f32[1,5,16,256]{3,2,1,0:T(8,128)S(1)}, f32[2,16,256]{2,1,0:T(8,128)S(1)}, f32[8,128]{1,0:T(8,128)S(1)}) custom-call(s32[1,2048]{1,0:T(1,128)} %bitcast.8, s32[16,128]{1,0:T(8,128)} %bitcast.9, f32[16,128]{1,0:T(8,128)} %bitcast.10, f32[16,128]{1,0:T(8,128)} %bitcast.11, s32[5,5]{1,0:T(8,128)} %mask_hbm.1, ...), custom_call_target="tpu_custom_call" | custom-call | tf_op jit(solution)/shard_map/prep/pallas_call | solution.py:512
  1.9 0.0 collective-permute-done.1.vel_other_ref
  1.9 0.0 collective-permute-done.other_ref
  1.9 0.1 iota.7.place_ref
  2.0 1.8 %forecast.1 = f32[416,128]{1,0:T(8,128)} custom-call(f32[8,128]{1,0:T(8,128)S(1)} %iota.7.place_ref, f32[8,128]{1,0:T(8,128)S(1)} %get-tuple-element.14.kappa_ref, f32[1,5,16,256]{3,2,1,0:T(8,128)S(1)} %get-tuple-element.15.own_ref, f32[1,5,16,256]{3,2,1,0:T(8,128)S(1)} %collective-permute-done.other_ref, f32[2,16,256]{2,1,0:T(8,128)S(1)} %get-tuple-element.16.vel_own_ref, ...), custom_call_target="tpu_custom_call" | custom-call | tf_op jit(solution)/shard_map/forecast/pallas_call | solution.py:544
  3.8 8.3 %all-to-all-start = ((f32[16,26,1,128]{3,2,1,0:T(1,128)}), f32[16,26,1,128]{3,2,1,0:T(1,128)S(1)}, u32[]{:S(2)}, u32[]{:S(2)}) async-start(f32[16,26,1,128]{3,2,1,0:T(1,128)} %bitcast.5), calls=%async_computation | async-start | bytes 425984 | tf_op jit(solution)/shard_map/all_to_all | solution.py:556
  12.2 6.6 %localize.1 = (bf16[1024,1024]{1,0:T(8,128)(2,1)S(1)}, bf16[512,1024]{1,0:T(8,128)(2,1)S(1)}, bf16[512,1024]{1,0:T(8,128)(2,1)}, bf16[2048,256]{1,0:T(8,128)(2,1)}, bf16[2048,256]{1,0:T(8,128)(2,1)}) custom-call(f32[8,128]{1,0:T(8,128)S(1)} %iota.7.place_ref, f32[16,2048]{1,0:T(8,128)S(1)} %get-tuple-element.17.info_ref), custom_call_target="tpu_custom_call" | custom-call | tf_op jit(solution)/shard_map/localize/pallas_call | solution.py:562
  18.7 2.6 %all-to-all-done = f32[16,26,1,128]{3,2,1,0:T(1,128)S(1)} async-done(((f32[16,26,1,128]{3,2,1,0:T(1,128)}), f32[16,26,1,128]{3,2,1,0:T(1,128)S(1)}, u32[]{:S(2)}, u32[]{:S(2)}) %all-to-all-start) | async-done | bytes 213024 | tf_op jit(solution)/shard_map/all_to_all | solution.py:556
  21.3 5.4 %update.1 = f32[16,5,1,1,256]{4,3,2,1,0:T(1,128)} custom-call(f32[416,128]{1,0:T(8,128)S(1)} %bitcast.7, f32[16,2048]{1,0:T(8,128)S(1)} %get-tuple-element.17.info_ref, bf16[1024,1024]{1,0:T(8,128)(2,1)S(1)} %get-tuple-element.18.pair_hi_ref, bf16[512,1024]{1,0:T(8,128)(2,1)S(1)} %get-tuple-element.19.pair_lo_ref, ...), custom_call_target="tpu_custom_call" | custom-call | tf_op jit(solution)/shard_map/update/pallas_call | solution.py:585
  (1 shorter events, 0.0 us)
Async XLA Ops:
  0.0 1.9 %collective-permute-start.1 = (f32[2,16,256]{2,1,0:T(8,128)}, f32[2,16,256]{2,1,0:T(8,128)S(1)}, u32[]{:S(2)}, u32[]{:S(2)}) collective-permute-start(f32[2,16,256]{2,1,0:T(8,128)} %velocity_hbm.1), channel_id=1, source_target_pairs={{0,1},{1,0},{2,3},{3,2},{4,5},{5,4},{6,7},{7,6},{8,9},{9,8},{10,11... | collective-permute-start | bytes 98312 | tf_op jit(solution)/shard_map/ppermute | solution.py:510
  0.5 1.5 %collective-permute-start = (f32[1,5,16,256]{3,2,1,0:T(8,128)}, f32[1,5,16,256]{3,2,1,0:T(8,128)S(1)}, u32[]{:S(2)}, u32[]{:S(2)}) collective-permute-start(f32[1,5,16,256]{3,2,1,0:T(8,128)} %stack_hbm.1), channel_id=1, source_target_pairs={{0,1},{1,0},{2,3},{3,2},{4,5},{5,4},{6,7},{7,6},{8,9},{9,8},{10,11... | collective-permute-start | bytes 245768 | tf_op jit(solution)/shard_map/ppermute | solution.py:509
  3.8 17.5 %all-to-all-start = ((f32[16,26,1,128]{3,2,1,0:T(1,128)}), f32[16,26,1,128]{3,2,1,0:T(1,128)S(1)}, u32[]{:S(2)}, u32[]{:S(2)}) async-start(f32[16,26,1,128]{3,2,1,0:T(1,128)} %bitcast.5), calls=%async_computation | async-start | bytes 425984 | tf_op jit(solution)/shard_map/all_to_all | solution.py:556

commit v4 on v3

--- a/solution.py
+++ b/solution.py
@@ -243,21 +243,28 @@
     u_pos, u_neg = jnp.maximum(u, 0.0), jnp.minimum(u, 0.0)
     v_pos, v_neg = jnp.maximum(v, 0.0), jnp.minimum(v, 0.0)
     outflow = (u_neg - u_pos) + (v_neg - v_pos)
+    cells, weights = [], []
     for f in range(n_fields):
         kappa = kappa_ref[f : f + 1, 0:1]
-        k_c = (1.0 - 4.0 * kappa) + outflow
-        k_n = jnp.where(row == 0, 0.0, kappa + v_pos)
-        k_s = jnp.where(row == n_rows - 1, 0.0, kappa - v_neg)
-        k_w = jnp.where(col == 0, 0.0, kappa + u_pos)
-        k_e = jnp.where(col == n_cols - 1, 0.0, kappa - u_neg)
-        c = whole_of(own_ref[0, f], other_ref[0, f])
-        for _ in range(SUBSTEPS):
-            c = (
+        weights.append((
+            (1.0 - 4.0 * kappa) + outflow,
+            jnp.where(row == 0, 0.0, kappa + v_pos),
+            jnp.where(row == n_rows - 1, 0.0, kappa - v_neg),
+            jnp.where(col == 0, 0.0, kappa + u_pos),
+            jnp.where(col == n_cols - 1, 0.0, kappa - u_neg),
+        ))
+        cells.append(whole_of(own_ref[0, f], other_ref[0, f]))
+    for _ in range(SUBSTEPS):
+        for f in range(n_fields):
+            c = cells[f]
+            k_c, k_n, k_s, k_w, k_e = weights[f]
+            cells[f] = (
                 (c * k_c + pltpu.roll(c, 1, 0) * k_n)
                 + (pltpu.roll(c, n_rows - 1, 0) * k_s + pltpu.roll(c, 1, 1) * k_w)
                 + pltpu.roll(c, n_cols - 1, 1) * k_e
             )
-        field_buf[f] = c
+    for f in range(n_fields):
+        field_buf[f] = cells[f]
     whole = field_buf[...].reshape(n_fields * n_rows, n_cols)
     strips = n_fields * n_rows
     parts = jnp.concatenate(split_three(whole), axis=0)
@@ -390,21 +397,22 @@
     variance = jnp.sum(anomaly * anomaly, axis=0, keepdims=True) * (1.0 / (members - 1)) + var
     root = jnp.sqrt(variance)
     shrunk = anomaly * (1.0 / ((members - 1) * (root * (jnp.sqrt(var) + root))))
-    rows = [shrunk * member_roll(anomaly, -d) for d in range(members // 2 + 1)]
+    rows = [shrunk * member_roll(anomaly, -d) for d in range(members // 2)]
     rows.append(anomaly * ((value - average) / ((members - 1) * variance)))
     return rows
 
 
 def combined(state, sums):
     members = state.shape[0]
+    half = members // 2
     centred = state - jnp.sum(state, axis=0, keepdims=True) * (1.0 / members)
-    offsets = members // 2
     block = lambda d: sums[d * members : (d + 1) * members]
-    move = centred * block(0) + member_roll(centred, -offsets) * block(offsets)
-    for d in range(1, offsets):
-        move = move + member_roll(centred, -d) * block(d)
-        move = move + member_roll(centred * block(d), d)
-    shift = jnp.sum(centred * block(offsets + 1), axis=0, keepdims=True)
+    across = member_roll(centred, half)
+    move = (centred - across) * block(0)
+    for d in range(1, half):
+        move = move + (member_roll(centred, -d) - across) * block(d)
+        move = move + member_roll((centred - member_roll(across, -d)) * block(d), d)
+    shift = jnp.sum(centred * block(half), axis=0, keepdims=True)
     return state + (shift - move)
 
 
@@ -438,39 +446,44 @@
             fac_buf[b, i * members : (i + 1) * members, :] = high
             fac_buf[b, size + i * members : size + (i + 1) * members, :] = low
 
-    @pl.when(pl.program_id(0) == 0)
-    def _():
-        for copy in copies:
-            copy.start()
-        set_factors(0, priors_of(0))
-        first = bdot(fac_buf[0], pair_hi_ref[...])
-        sums_buf[...] = (first[:size] + first[size:]) + bdot(fac_buf[0, :size, :kept], pair_lo_ref[...])
-
-    @pl.when(pl.program_id(0) == 1)
-    def _():
-        finish(copies[:1])
-        sums = sums_buf[...] + bdot(fac_buf[0, :size, kept:], rest_ref[...])
-        set_factors(1, combined(priors_of(1), sums))
-
-    @pl.when(pl.program_id(0) == 2)
-    def _():
-        finish(copies[1:])
-        states = [
-            jnp.concatenate([member_row(f * pieces + h) for h in range(pieces)], axis=1)
-            for f in range(n_fields)
-        ]
-        all_rows = n_fields * size
-        for b in range(BATCHES):
-            span = slice(b * batch, (b + 1) * batch)
+    def run(step, carry):
+        @pl.when(step == 0)
+        def _():
+            for copy in copies:
+                copy.start()
+            set_factors(0, priors_of(0))
+            first = bdot(fac_buf[0], pair_hi_ref[...])
+            sums_buf[...] = (first[:size] + first[size:]) + bdot(fac_buf[0, :size, :kept], pair_lo_ref[...])
+
+        @pl.when(step == 1)
+        def _():
+            finish(copies[:1])
+            sums = sums_buf[...] + bdot(fac_buf[0, :size, kept:], rest_ref[...])
+            set_factors(1, combined(priors_of(1), sums))
+
+        @pl.when(step == 2)
+        def _():
+            finish(copies[1:])
+            states = [
+                jnp.concatenate([member_row(f * pieces + h) for h in range(pieces)], axis=1)
+                for f in range(n_fields)
+            ]
+            all_rows = n_fields * size
+            for b in range(BATCHES):
+                span = slice(b * batch, (b + 1) * batch)
+                for f in range(n_fields):
+                    open_to = info_ref[8 + f : 9 + f, span].astype(jnp.bfloat16)
+                    mask_buf[f * size : (f + 1) * size, :] = fac_buf[b, :size, :] * open_to
+                    mask_buf[all_rows + f * size : all_rows + (f + 1) * size, :] = fac_buf[b, size:, :] * open_to
+                first = bdot(mask_buf[...], cell_hi_ref[span, :])
+                sums = (first[:all_rows] + first[all_rows:]) + bdot(mask_buf[:all_rows, :], cell_lo_ref[span, :])
+                states = [combined(state, sums[f * size : (f + 1) * size]) for f, state in enumerate(states)]
             for f in range(n_fields):
-                open_to = info_ref[8 + f : 9 + f, span].astype(jnp.bfloat16)
-                mask_buf[f * size : (f + 1) * size, :] = fac_buf[b, :size, :] * open_to
-                mask_buf[all_rows + f * size : all_rows + (f + 1) * size, :] = fac_buf[b, size:, :] * open_to
-            first = bdot(mask_buf[...], cell_hi_ref[span, :])
-            sums = (first[:all_rows] + first[all_rows:]) + bdot(mask_buf[:all_rows, :], cell_lo_ref[span, :])
-            states = [combined(state, sums[f * size : (f + 1) * size]) for f, state in enumerate(states)]
-        for f in range(n_fields):
-            out_ref[:, f, 0, 0, :] = states[f]
+                out_ref[:, f, 0, 0, :] = states[f]
+
+        return carry
+
+    lax.fori_loop(0, 3, run, 0)
 
 
 def vmem_spec():
@@ -581,10 +594,9 @@
         compiler_params=params,
         name="localize",
     )(place, info)
-    rows = n_mem * (n_mem // 2 + 2)
+    rows = n_mem * (n_mem // 2 + 1)
     return pl.pallas_call(
         functools.partial(update_kernel, members=n_mem, n_fields=n_fields),
-        grid=(3,),
         out_shape=shape((n_mem, n_fields, 1, 1, n_cols), f32),
         in_specs=[vmem_spec()] * 4 + [hbm_spec()] * 3,
         out_specs=vmem_spec(),

time: 27.1 us -> 26.9 us (level)
  no operation moved by 1% of the time
where the time goes in v4:
time: 26.9 us; the launch traced here: 26.6 us
  Pallas kernels  15 us (56%)
  starting transfers between devices  8.81 us (33%)
  waiting for transfers between devices  2.65 us (10%)
    all_to_all x1, starting transfers between devices, quick_device(): lax.all_to_all(send.reshape(n_mem, chunk, 1, LANES), 'mem', split_axis=0,...  8.3 us
    pallas_call x1, Pallas kernels, quick_device(): pl.pallas_call(loc_kernel, out_shape=(shape((batch, n_pair), bf16), shape...  6.55 us
    pallas_call x1, Pallas kernels, quick_device(): pl.pallas_call(functools.partial(update_kernel, members=n_mem, n_fields=n...  5.27 us
    all_to_all x1, waiting for transfers between devices, quick_device(): lax.all_to_all(send.reshape(n_mem, chunk, 1, LANES), 'mem', split_axis=0,...  2.62 us
    pallas_call x1, Pallas kernels, quick_device(): pl.pallas_call(forecast_kernel, out_shape=shape((n_mem * chunk, LANES), f...  1.83 us
    pallas_call x1, Pallas kernels, quick_device(): pl.pallas_call(functools.partial(prep_kernel, total_rows=total_rows, n_co...  1.38 us
  transfers between devices with their start and end apart: 3, of which 1 were waited for; matrix products, arithmetic and copies ran while one was open for 0% of the time, Pallas kernels for 30%

profile of v4, /device:TPU:0, one launch (start us, length us, event | category | flops | bytes accessed | tf_op | source)
XLA Modules:
  0.0 26.6 jit_solution(6817049263723498947)
XLA Ops:
  0.0 0.5 %collective-permute-start.1 = (f32[2,16,256]{2,1,0:T(8,128)}, f32[2,16,256]{2,1,0:T(8,128)S(1)}, u32[]{:S(2)}, u32[]{:S(2)}) collective-permute-start(f32[2,16,256]{2,1,0:T(8,128)} %velocity_hbm.1), channel_id=1, source_target_pairs={{0,1},{1,0},{2,3},{3,2},{4,5},{5,4},{6,7},{7,6},{8,9},{9,8},{10,11... | collective-permute-start | bytes 98312 | tf_op jit(solution)/shard_map/ppermute | solution.py:523
  0.5 0.1 collective-permute-start
  0.5 1.4 %prep.1 = (f32[16,2048]{1,0:T(8,128)S(1)}, f32[1,5,16,256]{3,2,1,0:T(8,128)S(1)}, f32[2,16,256]{2,1,0:T(8,128)S(1)}, f32[8,128]{1,0:T(8,128)S(1)}) custom-call(s32[1,2048]{1,0:T(1,128)} %bitcast.8, s32[16,128]{1,0:T(8,128)} %bitcast.9, f32[16,128]{1,0:T(8,128)} %bitcast.10, f32[16,128]{1,0:T(8,128)} %bitcast.11, s32[5,5]{1,0:T(8,128)} %mask_hbm.1, ...), custom_call_target="tpu_custom_call" | custom-call | tf_op jit(solution)/shard_map/prep/pallas_call | solution.py:525
  1.9 0.0 collective-permute-done.1.vel_other_ref
  1.9 0.0 collective-permute-done.other_ref
  1.9 0.1 iota.7.place_ref
  2.0 1.8 %forecast.1 = f32[416,128]{1,0:T(8,128)} custom-call(f32[8,128]{1,0:T(8,128)S(1)} %iota.7.place_ref, f32[8,128]{1,0:T(8,128)S(1)} %get-tuple-element.14.kappa_ref, f32[1,5,16,256]{3,2,1,0:T(8,128)S(1)} %get-tuple-element.15.own_ref, f32[1,5,16,256]{3,2,1,0:T(8,128)S(1)} %collective-permute-done.other_ref, f32[2,16,256]{2,1,0:T(8,128)S(1)} %get-tuple-element.16.vel_own_ref, ...), custom_call_target="tpu_custom_call" | custom-call | tf_op jit(solution)/shard_map/forecast/pallas_call | solution.py:557
  3.8 8.3 %all-to-all-start = ((f32[16,26,1,128]{3,2,1,0:T(1,128)}), f32[16,26,1,128]{3,2,1,0:T(1,128)S(1)}, u32[]{:S(2)}, u32[]{:S(2)}) async-start(f32[16,26,1,128]{3,2,1,0:T(1,128)} %bitcast.5), calls=%async_computation | async-start | bytes 425984 | tf_op jit(solution)/shard_map/all_to_all | solution.py:569
  12.2 6.6 %localize.1 = (bf16[1024,1024]{1,0:T(8,128)(2,1)S(1)}, bf16[512,1024]{1,0:T(8,128)(2,1)S(1)}, bf16[512,1024]{1,0:T(8,128)(2,1)}, bf16[2048,256]{1,0:T(8,128)(2,1)}, bf16[2048,256]{1,0:T(8,128)(2,1)}) custom-call(f32[8,128]{1,0:T(8,128)S(1)} %iota.7.place_ref, f32[16,2048]{1,0:T(8,128)S(1)} %get-tuple-element.17.info_ref), custom_call_target="tpu_custom_call" | custom-call | tf_op jit(solution)/shard_map/localize/pallas_call | solution.py:575
  18.7 2.6 %all-to-all-done = f32[16,26,1,128]{3,2,1,0:T(1,128)S(1)} async-done(((f32[16,26,1,128]{3,2,1,0:T(1,128)}), f32[16,26,1,128]{3,2,1,0:T(1,128)S(1)}, u32[]{:S(2)}, u32[]{:S(2)}) %all-to-all-start) | async-done | bytes 213024 | tf_op jit(solution)/shard_map/all_to_all | solution.py:569
  21.3 5.3 %update.1 = f32[16,5,1,1,256]{4,3,2,1,0:T(1,128)} custom-call(f32[416,128]{1,0:T(8,128)S(1)} %bitcast.7, f32[16,2048]{1,0:T(8,128)S(1)} %get-tuple-element.17.info_ref, bf16[1024,1024]{1,0:T(8,128)(2,1)S(1)} %get-tuple-element.18.pair_hi_ref, bf16[512,1024]{1,0:T(8,128)(2,1)S(1)} %get-tuple-element.19.pair_lo_ref, ...), custom_call_target="tpu_custom_call" | custom-call | tf_op jit(solution)/shard_map/update/pallas_call | solution.py:598
  (1 shorter events, 0.0 us)
Async XLA Ops:
  0.0 1.9 %collective-permute-start.1 = (f32[2,16,256]{2,1,0:T(8,128)}, f32[2,16,256]{2,1,0:T(8,128)S(1)}, u32[]{:S(2)}, u32[]{:S(2)}) collective-permute-start(f32[2,16,256]{2,1,0:T(8,128)} %velocity_hbm.1), channel_id=1, source_target_pairs={{0,1},{1,0},{2,3},{3,2},{4,5},{5,4},{6,7},{7,6},{8,9},{9,8},{10,11... | collective-permute-start | bytes 98312 | tf_op jit(solution)/shard_map/ppermute | solution.py:523
  0.5 1.5 %collective-permute-start = (f32[1,5,16,256]{3,2,1,0:T(8,128)}, f32[1,5,16,256]{3,2,1,0:T(8,128)S(1)}, u32[]{:S(2)}, u32[]{:S(2)}) collective-permute-start(f32[1,5,16,256]{3,2,1,0:T(8,128)} %stack_hbm.1), channel_id=1, source_target_pairs={{0,1},{1,0},{2,3},{3,2},{4,5},{5,4},{6,7},{7,6},{8,9},{9,8},{10,11... | collective-permute-start | bytes 245768 | tf_op jit(solution)/shard_map/ppermute | solution.py:522
  3.8 17.5 %all-to-all-start = ((f32[16,26,1,128]{3,2,1,0:T(1,128)}), f32[16,26,1,128]{3,2,1,0:T(1,128)S(1)}, u32[]{:S(2)}, u32[]{:S(2)}) async-start(f32[16,26,1,128]{3,2,1,0:T(1,128)} %bitcast.5), calls=%async_computation | async-start | bytes 425984 | tf_op jit(solution)/shard_map/all_to_all | solution.py:569

commit v5 on v4

--- a/solution.py
+++ b/solution.py
@@ -159,6 +159,11 @@
 def finish(copies):
     for copy in copies:
         copy.wait()
+
+
+def half_turn(x):
+    half = x.shape[0] // 2
+    return jnp.concatenate([x[half:], x[:half]], axis=0)
 
 
 def prep_kernel(
@@ -288,7 +293,7 @@
         send_ref[d * chunk + lead : (d + 1) * chunk, :] = priors
     pieces = n_cols // LANES
     for f in range(n_fields):
-        rows = jnp.where(first_slab, field_buf[f, :half, :], field_buf[f, half:, :])
+        rows = half_turn(jnp.where(first_slab, field_buf[f, :half, :], field_buf[f, half:, :]))
         for h in range(pieces):
             send_ref[pl.ds(f * pieces + h, n_dest, stride=chunk), :] = rows[
                 :, h * LANES : (h + 1) * LANES
@@ -479,7 +484,7 @@
                 sums = (first[:all_rows] + first[all_rows:]) + bdot(mask_buf[:all_rows, :], cell_lo_ref[span, :])
                 states = [combined(state, sums[f * size : (f + 1) * size]) for f, state in enumerate(states)]
             for f in range(n_fields):
-                out_ref[:, f, 0, 0, :] = states[f]
+                out_ref[:, f, 0, 0, :] = half_turn(states[f])
 
         return carry
 
@@ -567,7 +572,12 @@
         name="forecast",
     )(place, kappa, own, other, vel_own, vel_other, info)
     recv = lax.all_to_all(
-        send.reshape(n_mem, chunk, 1, LANES), "mem", split_axis=0, concat_axis=0, tiled=True
+        send.reshape(n_mem, chunk, 1, LANES),
+        "mem",
+        split_axis=0,
+        concat_axis=0,
+        axis_index_groups=[[(i + n_mem // 2) % n_mem for i in range(n_mem)]],
+        tiled=True,
     ).reshape(send.shape)
     n_pair = n_obs - batch
     bf16 = jnp.bfloat16

time: 26.9 us -> 25.1 us (0.933)
  waiting for transfers between devices: 2.65 us -> 0.39 us
  starting transfers between devices: 8.81 us -> 9.28 us
    all_to_all x1, waiting for transfers between devices: 2.62 us -> 0.36 us  [quick_device(): lax.all_to_all(send.reshape(n_mem, chunk, 1, LANES), 'mem', split_axis=0,...]
    all_to_all x1, starting transfers between devices: 8.3 us -> 8.77 us  [quick_device(): lax.all_to_all(send.reshape(n_mem, chunk, 1, LANES), 'mem', split_axis=0,...]
  transfers between devices with their start and end apart: 3 -> 3, of which waited for: 1 -> 1; matrix products, arithmetic and copies ran while one was open for 0% -> 0% of each run, Pallas kernels for 30% -> 32%
where the time goes in v5:
time: 25.1 us; the launch traced here: 24.8 us
  Pallas kernels  15 us (60%)
  starting transfers between devices  9.28 us (37%)
  waiting for transfers between devices  0.39 us (2%)
    all_to_all x1, starting transfers between devices, quick_device(): lax.all_to_all(send.reshape(n_mem, chunk, 1, LANES), 'mem', split_axis=0,...  8.77 us
    pallas_call x1, Pallas kernels, quick_device(): pl.pallas_call(loc_kernel, out_shape=(shape((batch, n_pair), bf16), shape...  6.54 us
    pallas_call x1, Pallas kernels, quick_device(): pl.pallas_call(functools.partial(update_kernel, members=n_mem, n_fields=n...  5.27 us
    pallas_call x1, Pallas kernels, quick_device(): pl.pallas_call(forecast_kernel, out_shape=shape((n_mem * chunk, LANES), f...  1.83 us
    pallas_call x1, Pallas kernels, quick_device(): pl.pallas_call(functools.partial(prep_kernel, total_rows=total_rows, n_co...  1.38 us
  transfers between devices with their start and end apart: 3, of which 1 were waited for; matrix products, arithmetic and copies ran while one was open for 0% of the time, Pallas kernels for 32%

profile of v5, /device:TPU:0, one launch (start us, length us, event | category | flops | bytes accessed | tf_op | source)
XLA Modules:
  0.0 24.8 jit_solution(1955216464513112645)
XLA Ops:
  0.0 0.5 %collective-permute-start.1 = (f32[2,16,256]{2,1,0:T(8,128)}, f32[2,16,256]{2,1,0:T(8,128)S(1)}, u32[]{:S(2)}, u32[]{:S(2)}) collective-permute-start(f32[2,16,256]{2,1,0:T(8,128)} %velocity_hbm.1), channel_id=1, source_target_pairs={{0,1},{1,0},{2,3},{3,2},{4,5},{5,4},{6,7},{7,6},{8,9},{9,8},{10,11... | collective-permute-start | bytes 98312 | tf_op jit(solution)/shard_map/ppermute | solution.py:528
  0.5 0.1 collective-permute-start
  0.5 1.4 %prep.1 = (f32[16,2048]{1,0:T(8,128)S(1)}, f32[1,5,16,256]{3,2,1,0:T(8,128)S(1)}, f32[2,16,256]{2,1,0:T(8,128)S(1)}, f32[8,128]{1,0:T(8,128)S(1)}) custom-call(s32[1,2048]{1,0:T(1,128)} %bitcast.8, s32[16,128]{1,0:T(8,128)} %bitcast.9, f32[16,128]{1,0:T(8,128)} %bitcast.10, f32[16,128]{1,0:T(8,128)} %bitcast.11, s32[5,5]{1,0:T(8,128)} %mask_hbm.1, ...), custom_call_target="tpu_custom_call" | custom-call | tf_op jit(solution)/shard_map/prep/pallas_call | solution.py:530
  1.9 0.0 collective-permute-done.1.vel_other_ref
  1.9 0.0 collective-permute-done.other_ref
  1.9 0.1 iota.7.place_ref
  2.0 1.8 %forecast.1 = f32[416,128]{1,0:T(8,128)} custom-call(f32[8,128]{1,0:T(8,128)S(1)} %iota.7.place_ref, f32[8,128]{1,0:T(8,128)S(1)} %get-tuple-element.14.kappa_ref, f32[1,5,16,256]{3,2,1,0:T(8,128)S(1)} %get-tuple-element.15.own_ref, f32[1,5,16,256]{3,2,1,0:T(8,128)S(1)} %collective-permute-done.other_ref, f32[2,16,256]{2,1,0:T(8,128)S(1)} %get-tuple-element.16.vel_own_ref, ...), custom_call_target="tpu_custom_call" | custom-call | tf_op jit(solution)/shard_map/forecast/pallas_call | solution.py:562
  3.8 8.8 %all-to-all-start = ((f32[16,26,1,128]{3,2,1,0:T(1,128)}), f32[16,26,1,128]{3,2,1,0:T(1,128)S(1)}, u32[]{:S(2)}, u32[]{:S(2)}) async-start(f32[16,26,1,128]{3,2,1,0:T(1,128)} %bitcast.5), calls=%async_computation | async-start | bytes 425984 | tf_op jit(solution)/shard_map/all_to_all | solution.py:574
  12.6 6.5 %localize.1 = (bf16[1024,1024]{1,0:T(8,128)(2,1)S(1)}, bf16[512,1024]{1,0:T(8,128)(2,1)S(1)}, bf16[512,1024]{1,0:T(8,128)(2,1)}, bf16[2048,256]{1,0:T(8,128)(2,1)}, bf16[2048,256]{1,0:T(8,128)(2,1)}) custom-call(f32[8,128]{1,0:T(8,128)S(1)} %iota.7.place_ref, f32[16,2048]{1,0:T(8,128)S(1)} %get-tuple-element.17.info_ref), custom_call_target="tpu_custom_call" | custom-call | tf_op jit(solution)/shard_map/localize/pallas_call | solution.py:585
  19.2 0.4 %all-to-all-done = f32[16,26,1,128]{3,2,1,0:T(1,128)S(1)} async-done(((f32[16,26,1,128]{3,2,1,0:T(1,128)}), f32[16,26,1,128]{3,2,1,0:T(1,128)S(1)}, u32[]{:S(2)}, u32[]{:S(2)}) %all-to-all-start) | async-done | bytes 213024 | tf_op jit(solution)/shard_map/all_to_all | solution.py:574
  19.5 5.3 %update.1 = f32[16,5,1,1,256]{4,3,2,1,0:T(1,128)} custom-call(f32[416,128]{1,0:T(8,128)S(1)} %bitcast.7, f32[16,2048]{1,0:T(8,128)S(1)} %get-tuple-element.17.info_ref, bf16[1024,1024]{1,0:T(8,128)(2,1)S(1)} %get-tuple-element.18.pair_hi_ref, bf16[512,1024]{1,0:T(8,128)(2,1)S(1)} %get-tuple-element.19.pair_lo_ref, ...), custom_call_target="tpu_custom_call" | custom-call | tf_op jit(solution)/shard_map/update/pallas_call | solution.py:608
  (1 shorter events, 0.0 us)
Async XLA Ops:
  0.0 1.9 %collective-permute-start.1 = (f32[2,16,256]{2,1,0:T(8,128)}, f32[2,16,256]{2,1,0:T(8,128)S(1)}, u32[]{:S(2)}, u32[]{:S(2)}) collective-permute-start(f32[2,16,256]{2,1,0:T(8,128)} %velocity_hbm.1), channel_id=1, source_target_pairs={{0,1},{1,0},{2,3},{3,2},{4,5},{5,4},{6,7},{7,6},{8,9},{9,8},{10,11... | collective-permute-start | bytes 98312 | tf_op jit(solution)/shard_map/ppermute | solution.py:528
  0.5 1.5 %collective-permute-start = (f32[1,5,16,256]{3,2,1,0:T(8,128)}, f32[1,5,16,256]{3,2,1,0:T(8,128)S(1)}, u32[]{:S(2)}, u32[]{:S(2)}) collective-permute-start(f32[1,5,16,256]{3,2,1,0:T(8,128)} %stack_hbm.1), channel_id=1, source_target_pairs={{0,1},{1,0},{2,3},{3,2},{4,5},{5,4},{6,7},{7,6},{8,9},{9,8},{10,11... | collective-permute-start | bytes 245768 | tf_op jit(solution)/shard_map/ppermute | solution.py:527
  3.8 15.7 %all-to-all-start = ((f32[16,26,1,128]{3,2,1,0:T(1,128)}), f32[16,26,1,128]{3,2,1,0:T(1,128)S(1)}, u32[]{:S(2)}, u32[]{:S(2)}) async-start(f32[16,26,1,128]{3,2,1,0:T(1,128)} %bitcast.5), calls=%async_computation | async-start | bytes 425984 | tf_op jit(solution)/shard_map/all_to_all | solution.py:574

commit v6 on v5

--- a/solution.py
+++ b/solution.py
@@ -161,9 +161,8 @@
         copy.wait()
 
 
-def half_turn(x):
-    half = x.shape[0] // 2
-    return jnp.concatenate([x[half:], x[:half]], axis=0)
+def exchange_order(n):
+    return [(n // 2 - 1 - i) % n for i in range(n)]
 
 
 def prep_kernel(
@@ -293,11 +292,11 @@
         send_ref[d * chunk + lead : (d + 1) * chunk, :] = priors
     pieces = n_cols // LANES
     for f in range(n_fields):
-        rows = half_turn(jnp.where(first_slab, field_buf[f, :half, :], field_buf[f, half:, :]))
-        for h in range(pieces):
-            send_ref[pl.ds(f * pieces + h, n_dest, stride=chunk), :] = rows[
-                :, h * LANES : (h + 1) * LANES
-            ]
+        rows = jnp.where(first_slab, field_buf[f, :half, :], field_buf[f, half:, :])
+        for i, dest in enumerate(exchange_order(n_dest)):
+            for h in range(pieces):
+                at = i * chunk + f * pieces + h
+                send_ref[at : at + 1, :] = rows[dest : dest + 1, h * LANES : (h + 1) * LANES]
     for i in range(n_fields * pieces, lead):
         send_ref[pl.ds(i, n_dest, stride=chunk), :] = jnp.zeros((n_dest, LANES), jnp.float32)
 
@@ -343,15 +342,15 @@
     own_row = place_ref[1:2, 0:1]
     gap_row = (lax.broadcasted_iota(jnp.int32, (table_rows, LANES), 0).astype(jnp.float32) - own_row) * scale
     gap_col = lax.broadcasted_iota(jnp.int32, (table_rows, LANES), 1).astype(jnp.float32) * scale
-    high, mid, low = split_three(closeness_of(gap_row * gap_row + gap_col * gap_col))
-    row_ids = lax.broadcasted_iota(jnp.int32, (1, table_rows), 1)
+    by_row = jnp.concatenate(split_three(closeness_of(gap_row * gap_row + gap_col * gap_col)), axis=0)
+    row_ids = lax.broadcasted_iota(jnp.int32, (1, 3 * table_rows), 1) & (table_rows - 1)
     copies = []
     col_at, row_at = 7, terms
     for b in range(BATCHES):
         span = slice(b * batch, (b + 1) * batch)
         rows = infot_ref[span, row_at : row_at + 1].astype(jnp.int32)
         hot = (row_ids == rows).astype(jnp.float32).astype(jnp.bfloat16)
-        table = (bdot(hot, high) + bdot(hot, mid)) + bdot(hot, low)
+        table = bdot(hot, by_row)
         cols = infot_ref[span, col_at : col_at + 1] * -0.5
         col_k = jnp.broadcast_to(cols, (batch, LANES)).astype(jnp.int32)
         for h in range(n_cols // LANES):
@@ -484,7 +483,8 @@
                 sums = (first[:all_rows] + first[all_rows:]) + bdot(mask_buf[:all_rows, :], cell_lo_ref[span, :])
                 states = [combined(state, sums[f * size : (f + 1) * size]) for f, state in enumerate(states)]
             for f in range(n_fields):
-                out_ref[:, f, 0, 0, :] = half_turn(states[f])
+                for i, member in enumerate(exchange_order(members)):
+                    out_ref[member, f, 0, :, :] = states[f][i : i + 1]
 
         return carry
 
@@ -576,7 +576,7 @@
         "mem",
         split_axis=0,
         concat_axis=0,
-        axis_index_groups=[[(i + n_mem // 2) % n_mem for i in range(n_mem)]],
+        axis_index_groups=[exchange_order(n_mem)],
         tiled=True,
     ).reshape(send.shape)
     n_pair = n_obs - batch

time: 25.1 us -> 24.8 us (0.988)
  no operation moved by 1% of the time
where the time goes in v6:
time: 24.8 us; the launch traced here: 24.5 us
  Pallas kernels  15 us (60%)
  starting transfers between devices  9.28 us (37%)
    all_to_all x1, starting transfers between devices, quick_device(): lax.all_to_all(send.reshape(n_mem, chunk, 1, LANES), 'mem', split_axis=0,...  8.77 us
    pallas_call x1, Pallas kernels, quick_device(): pl.pallas_call(loc_kernel, out_shape=(shape((batch, n_pair), bf16), shape...  6.51 us
    pallas_call x1, Pallas kernels, quick_device(): pl.pallas_call(functools.partial(update_kernel, members=n_mem, n_fields=n...  5.27 us
    pallas_call x1, Pallas kernels, quick_device(): pl.pallas_call(forecast_kernel, out_shape=shape((n_mem * chunk, LANES), f...  1.83 us
    pallas_call x1, Pallas kernels, quick_device(): pl.pallas_call(functools.partial(prep_kernel, total_rows=total_rows, n_co...  1.38 us
  transfers between devices with their start and end apart: 3, of which 1 were waited for; matrix products, arithmetic and copies ran while one was open for 0% of the time, Pallas kernels for 32%

profile of v6, /device:TPU:0, one launch (start us, length us, event | category | flops | bytes accessed | tf_op | source)
XLA Modules:
  0.0 24.5 jit_solution(16272646453822160480)
XLA Ops:
  0.0 0.5 %collective-permute-start.1 = (f32[2,16,256]{2,1,0:T(8,128)}, f32[2,16,256]{2,1,0:T(8,128)S(1)}, u32[]{:S(2)}, u32[]{:S(2)}) collective-permute-start(f32[2,16,256]{2,1,0:T(8,128)} %velocity_hbm.1), channel_id=1, source_target_pairs={{0,1},{1,0},{2,3},{3,2},{4,5},{5,4},{6,7},{7,6},{8,9},{9,8},{10,11... | collective-permute-start | bytes 98312 | tf_op jit(solution)/shard_map/ppermute | solution.py:528
  0.5 0.1 collective-permute-start
  0.5 1.4 %prep.1 = (f32[16,2048]{1,0:T(8,128)S(1)}, f32[1,5,16,256]{3,2,1,0:T(8,128)S(1)}, f32[2,16,256]{2,1,0:T(8,128)S(1)}, f32[8,128]{1,0:T(8,128)S(1)}) custom-call(s32[1,2048]{1,0:T(1,128)} %bitcast.8, s32[16,128]{1,0:T(8,128)} %bitcast.9, f32[16,128]{1,0:T(8,128)} %bitcast.10, f32[16,128]{1,0:T(8,128)} %bitcast.11, s32[5,5]{1,0:T(8,128)} %mask_hbm.1, ...), custom_call_target="tpu_custom_call" | custom-call | tf_op jit(solution)/shard_map/prep/pallas_call | solution.py:530
  1.9 0.0 collective-permute-done.1.vel_other_ref
  1.9 0.0 collective-permute-done.other_ref
  1.9 0.1 iota.7.place_ref
  2.0 1.8 %forecast.1 = f32[416,128]{1,0:T(8,128)} custom-call(f32[8,128]{1,0:T(8,128)S(1)} %iota.7.place_ref, f32[8,128]{1,0:T(8,128)S(1)} %get-tuple-element.14.kappa_ref, f32[1,5,16,256]{3,2,1,0:T(8,128)S(1)} %get-tuple-element.15.own_ref, f32[1,5,16,256]{3,2,1,0:T(8,128)S(1)} %collective-permute-done.other_ref, f32[2,16,256]{2,1,0:T(8,128)S(1)} %get-tuple-element.16.vel_own_ref, ...), custom_call_target="tpu_custom_call" | custom-call | tf_op jit(solution)/shard_map/forecast/pallas_call | solution.py:562
  3.8 8.8 %all-to-all-start = ((f32[16,26,1,128]{3,2,1,0:T(1,128)}), f32[16,26,1,128]{3,2,1,0:T(1,128)S(1)}, u32[]{:S(2)}, u32[]{:S(2)}) async-start(f32[16,26,1,128]{3,2,1,0:T(1,128)} %bitcast.5), calls=%async_computation | async-start | bytes 425984 | tf_op jit(solution)/shard_map/all_to_all | solution.py:574
  12.6 6.5 %localize.1 = (bf16[1024,1024]{1,0:T(8,128)(2,1)S(1)}, bf16[512,1024]{1,0:T(8,128)(2,1)S(1)}, bf16[512,1024]{1,0:T(8,128)(2,1)}, bf16[2048,256]{1,0:T(8,128)(2,1)}, bf16[2048,256]{1,0:T(8,128)(2,1)}) custom-call(f32[8,128]{1,0:T(8,128)S(1)} %iota.7.place_ref, f32[16,2048]{1,0:T(8,128)S(1)} %get-tuple-element.17.info_ref), custom_call_target="tpu_custom_call" | custom-call | tf_op jit(solution)/shard_map/localize/pallas_call | solution.py:585
  19.1 0.1 all-to-all-done
  19.2 5.3 %update.1 = f32[16,5,1,1,256]{4,3,2,1,0:T(1,128)} custom-call(f32[416,128]{1,0:T(8,128)S(1)} %bitcast.7, f32[16,2048]{1,0:T(8,128)S(1)} %get-tuple-element.17.info_ref, bf16[1024,1024]{1,0:T(8,128)(2,1)S(1)} %get-tuple-element.18.pair_hi_ref, bf16[512,1024]{1,0:T(8,128)(2,1)S(1)} %get-tuple-element.19.pair_lo_ref, ...), custom_call_target="tpu_custom_call" | custom-call | tf_op jit(solution)/shard_map/update/pallas_call | solution.py:608
  (1 shorter events, 0.0 us)
Async XLA Ops:
  0.0 1.9 %collective-permute-start.1 = (f32[2,16,256]{2,1,0:T(8,128)}, f32[2,16,256]{2,1,0:T(8,128)S(1)}, u32[]{:S(2)}, u32[]{:S(2)}) collective-permute-start(f32[2,16,256]{2,1,0:T(8,128)} %velocity_hbm.1), channel_id=1, source_target_pairs={{0,1},{1,0},{2,3},{3,2},{4,5},{5,4},{6,7},{7,6},{8,9},{9,8},{10,11... | collective-permute-start | bytes 98312 | tf_op jit(solution)/shard_map/ppermute | solution.py:528
  0.5 1.5 %collective-permute-start = (f32[1,5,16,256]{3,2,1,0:T(8,128)}, f32[1,5,16,256]{3,2,1,0:T(8,128)S(1)}, u32[]{:S(2)}, u32[]{:S(2)}) collective-permute-start(f32[1,5,16,256]{3,2,1,0:T(8,128)} %stack_hbm.1), channel_id=1, source_target_pairs={{0,1},{1,0},{2,3},{3,2},{4,5},{5,4},{6,7},{7,6},{8,9},{9,8},{10,11... | collective-permute-start | bytes 245768 | tf_op jit(solution)/shard_map/ppermute | solution.py:527
  3.8 15.4 %all-to-all-start = ((f32[16,26,1,128]{3,2,1,0:T(1,128)}), f32[16,26,1,128]{3,2,1,0:T(1,128)S(1)}, u32[]{:S(2)}, u32[]{:S(2)}) async-start(f32[16,26,1,128]{3,2,1,0:T(1,128)} %bitcast.5), calls=%async_computation | async-start | bytes 425984 | tf_op jit(solution)/shard_map/all_to_all | solution.py:574

commit v7 on v6

--- a/solution.py
+++ b/solution.py
@@ -162,7 +162,7 @@
 
 
 def exchange_order(n):
-    return [(n // 2 - 1 - i) % n for i in range(n)]
+    return [(i % 4 * (n // 4) + i // 4 + n // 2) % n for i in range(n)]
 
 
 def prep_kernel(

time: 24.8 us -> 24.7 us (level)
  transfers between devices with their start and end apart: 3 -> 3, of which waited for: 1 -> 0; matrix products, arithmetic and copies ran while one was open for 0% -> 0% of each run, Pallas kernels for 32% -> 32%
where the time goes in v7:
time: 24.7 us; the launch traced here: 24.4 us
  Pallas kernels  15 us (61%)
  starting transfers between devices  9.28 us (38%)
    all_to_all x1, starting transfers between devices, quick_device(): lax.all_to_all(send.reshape(n_mem, chunk, 1, LANES), 'mem', split_axis=0,...  8.77 us
    pallas_call x1, Pallas kernels, quick_device(): pl.pallas_call(loc_kernel, out_shape=(shape((batch, n_pair), bf16), shape...  6.51 us
    pallas_call x1, Pallas kernels, quick_device(): pl.pallas_call(functools.partial(update_kernel, members=n_mem, n_fields=n...  5.28 us
    pallas_call x1, Pallas kernels, quick_device(): pl.pallas_call(forecast_kernel, out_shape=shape((n_mem * chunk, LANES), f...  1.83 us
    pallas_call x1, Pallas kernels, quick_device(): pl.pallas_call(functools.partial(prep_kernel, total_rows=total_rows, n_co...  1.38 us
  transfers between devices with their start and end apart: 3, of which 0 were waited for; matrix products, arithmetic and copies ran while one was open for 0% of the time, Pallas kernels for 32%

profile of v7, /device:TPU:0, one launch (start us, length us, event | category | flops | bytes accessed | tf_op | source)
XLA Modules:
  0.0 24.4 jit_solution(9320360292592338899)
XLA Ops:
  0.0 0.5 %collective-permute-start.1 = (f32[2,16,256]{2,1,0:T(8,128)}, f32[2,16,256]{2,1,0:T(8,128)S(1)}, u32[]{:S(2)}, u32[]{:S(2)}) collective-permute-start(f32[2,16,256]{2,1,0:T(8,128)} %velocity_hbm.1), channel_id=1, source_target_pairs={{0,1},{1,0},{2,3},{3,2},{4,5},{5,4},{6,7},{7,6},{8,9},{9,8},{10,11... | collective-permute-start | bytes 98312 | tf_op jit(solution)/shard_map/ppermute | solution.py:528
  0.5 0.1 collective-permute-start
  0.5 1.4 %prep.1 = (f32[16,2048]{1,0:T(8,128)S(1)}, f32[1,5,16,256]{3,2,1,0:T(8,128)S(1)}, f32[2,16,256]{2,1,0:T(8,128)S(1)}, f32[8,128]{1,0:T(8,128)S(1)}) custom-call(s32[1,2048]{1,0:T(1,128)} %bitcast.8, s32[16,128]{1,0:T(8,128)} %bitcast.9, f32[16,128]{1,0:T(8,128)} %bitcast.10, f32[16,128]{1,0:T(8,128)} %bitcast.11, s32[5,5]{1,0:T(8,128)} %mask_hbm.1, ...), custom_call_target="tpu_custom_call" | custom-call | tf_op jit(solution)/shard_map/prep/pallas_call | solution.py:530
  1.9 0.0 collective-permute-done.1.vel_other_ref
  1.9 0.0 collective-permute-done.other_ref
  1.9 0.1 iota.7.place_ref
  2.0 1.8 %forecast.1 = f32[416,128]{1,0:T(8,128)} custom-call(f32[8,128]{1,0:T(8,128)S(1)} %iota.7.place_ref, f32[8,128]{1,0:T(8,128)S(1)} %get-tuple-element.14.kappa_ref, f32[1,5,16,256]{3,2,1,0:T(8,128)S(1)} %get-tuple-element.15.own_ref, f32[1,5,16,256]{3,2,1,0:T(8,128)S(1)} %collective-permute-done.other_ref, f32[2,16,256]{2,1,0:T(8,128)S(1)} %get-tuple-element.16.vel_own_ref, ...), custom_call_target="tpu_custom_call" | custom-call | tf_op jit(solution)/shard_map/forecast/pallas_call | solution.py:562
  3.8 8.8 %all-to-all-start = ((f32[16,26,1,128]{3,2,1,0:T(1,128)}), f32[16,26,1,128]{3,2,1,0:T(1,128)S(1)}, u32[]{:S(2)}, u32[]{:S(2)}) async-start(f32[16,26,1,128]{3,2,1,0:T(1,128)} %bitcast.5), calls=%async_computation | async-start | bytes 425984 | tf_op jit(solution)/shard_map/all_to_all | solution.py:574
  12.6 6.5 %localize.1 = (bf16[1024,1024]{1,0:T(8,128)(2,1)S(1)}, bf16[512,1024]{1,0:T(8,128)(2,1)S(1)}, bf16[512,1024]{1,0:T(8,128)(2,1)}, bf16[2048,256]{1,0:T(8,128)(2,1)}, bf16[2048,256]{1,0:T(8,128)(2,1)}) custom-call(f32[8,128]{1,0:T(8,128)S(1)} %iota.7.place_ref, f32[16,2048]{1,0:T(8,128)S(1)} %get-tuple-element.17.info_ref), custom_call_target="tpu_custom_call" | custom-call | tf_op jit(solution)/shard_map/localize/pallas_call | solution.py:585
  19.1 0.0 all-to-all-done
  19.1 5.3 %update.1 = f32[16,5,1,1,256]{4,3,2,1,0:T(1,128)} custom-call(f32[416,128]{1,0:T(8,128)S(1)} %bitcast.7, f32[16,2048]{1,0:T(8,128)S(1)} %get-tuple-element.17.info_ref, bf16[1024,1024]{1,0:T(8,128)(2,1)S(1)} %get-tuple-element.18.pair_hi_ref, bf16[512,1024]{1,0:T(8,128)(2,1)S(1)} %get-tuple-element.19.pair_lo_ref, ...), custom_call_target="tpu_custom_call" | custom-call | tf_op jit(solution)/shard_map/update/pallas_call | solution.py:608
  (1 shorter events, 0.0 us)
Async XLA Ops:
  0.0 1.9 %collective-permute-start.1 = (f32[2,16,256]{2,1,0:T(8,128)}, f32[2,16,256]{2,1,0:T(8,128)S(1)}, u32[]{:S(2)}, u32[]{:S(2)}) collective-permute-start(f32[2,16,256]{2,1,0:T(8,128)} %velocity_hbm.1), channel_id=1, source_target_pairs={{0,1},{1,0},{2,3},{3,2},{4,5},{5,4},{6,7},{7,6},{8,9},{9,8},{10,11... | collective-permute-start | bytes 98312 | tf_op jit(solution)/shard_map/ppermute | solution.py:528
  0.5 1.5 %collective-permute-start = (f32[1,5,16,256]{3,2,1,0:T(8,128)}, f32[1,5,16,256]{3,2,1,0:T(8,128)S(1)}, u32[]{:S(2)}, u32[]{:S(2)}) collective-permute-start(f32[1,5,16,256]{3,2,1,0:T(8,128)} %stack_hbm.1), channel_id=1, source_target_pairs={{0,1},{1,0},{2,3},{3,2},{4,5},{5,4},{6,7},{7,6},{8,9},{9,8},{10,11... | collective-permute-start | bytes 245768 | tf_op jit(solution)/shard_map/ppermute | solution.py:527
  3.8 15.3 %all-to-all-start = ((f32[16,26,1,128]{3,2,1,0:T(1,128)}), f32[16,26,1,128]{3,2,1,0:T(1,128)S(1)}, u32[]{:S(2)}, u32[]{:S(2)}) async-start(f32[16,26,1,128]{3,2,1,0:T(1,128)} %bitcast.5), calls=%async_computation | async-start | bytes 425984 | tf_op jit(solution)/shard_map/all_to_all | solution.py:574

commit v8 on v7

--- a/solution.py
+++ b/solution.py
@@ -271,7 +271,7 @@
         field_buf[f] = cells[f]
     whole = field_buf[...].reshape(n_fields * n_rows, n_cols)
     strips = n_fields * n_rows
-    parts = jnp.concatenate(split_three(whole), axis=0)
+    parts = jnp.concatenate(split_two(whole), axis=0)
     n_obs = info_ref.shape[1]
     width = 2 * LANES
     strip_ids = lax.broadcasted_iota(jnp.int32, (strips, width), 0)
@@ -281,7 +281,7 @@
         strip = info_ref[5:6, q * width : (q + 1) * width].astype(jnp.int32)
         hot = (col_ids == cols).astype(jnp.float32).astype(jnp.bfloat16)
         found = bdot(parts, hot)
-        found = (found[:strips] + found[strips : 2 * strips]) + found[2 * strips :]
+        found = found[:strips] + found[strips:]
         values = jnp.sum(jnp.where(strip_ids == strip, found, 0.0), axis=0, keepdims=True)
         for h in range(width // LANES):
             at = q * (width // LANES) + h

time: 24.7 us -> 24.6 us (level)
  no operation moved by 1% of the time
where the time goes in v8:
time: 24.6 us; the launch traced here: 24.3 us
  Pallas kernels  14.9 us (61%)
  starting transfers between devices  9.28 us (38%)
    all_to_all x1, starting transfers between devices, quick_device(): lax.all_to_all(send.reshape(n_mem, chunk, 1, LANES), 'mem', split_axis=0,...  8.77 us
    pallas_call x1, Pallas kernels, quick_device(): pl.pallas_call(loc_kernel, out_shape=(shape((batch, n_pair), bf16), shape...  6.52 us
    pallas_call x1, Pallas kernels, quick_device(): pl.pallas_call(functools.partial(update_kernel, members=n_mem, n_fields=n...  5.28 us
    pallas_call x1, Pallas kernels, quick_device(): pl.pallas_call(forecast_kernel, out_shape=shape((n_mem * chunk, LANES), f...  1.75 us
    pallas_call x1, Pallas kernels, quick_device(): pl.pallas_call(functools.partial(prep_kernel, total_rows=total_rows, n_co...  1.38 us
  transfers between devices with their start and end apart: 3, of which 0 were waited for; matrix products, arithmetic and copies ran while one was open for 0% of the time, Pallas kernels for 32%

profile of v8, /device:TPU:0, one launch (start us, length us, event | category | flops | bytes accessed | tf_op | source)
XLA Modules:
  0.0 24.3 jit_solution(11014633420876597800)
XLA Ops:
  0.0 0.5 %collective-permute-start.1 = (f32[2,16,256]{2,1,0:T(8,128)}, f32[2,16,256]{2,1,0:T(8,128)S(1)}, u32[]{:S(2)}, u32[]{:S(2)}) collective-permute-start(f32[2,16,256]{2,1,0:T(8,128)} %velocity_hbm.1), channel_id=1, source_target_pairs={{0,1},{1,0},{2,3},{3,2},{4,5},{5,4},{6,7},{7,6},{8,9},{9,8},{10,11... | collective-permute-start | bytes 98312 | tf_op jit(solution)/shard_map/ppermute | solution.py:528
  0.5 0.1 collective-permute-start
  0.5 1.4 %prep.1 = (f32[16,2048]{1,0:T(8,128)S(1)}, f32[1,5,16,256]{3,2,1,0:T(8,128)S(1)}, f32[2,16,256]{2,1,0:T(8,128)S(1)}, f32[8,128]{1,0:T(8,128)S(1)}) custom-call(s32[1,2048]{1,0:T(1,128)} %bitcast.8, s32[16,128]{1,0:T(8,128)} %bitcast.9, f32[16,128]{1,0:T(8,128)} %bitcast.10, f32[16,128]{1,0:T(8,128)} %bitcast.11, s32[5,5]{1,0:T(8,128)} %mask_hbm.1, ...), custom_call_target="tpu_custom_call" | custom-call | tf_op jit(solution)/shard_map/prep/pallas_call | solution.py:530
  1.9 0.0 collective-permute-done.1.vel_other_ref
  1.9 0.0 collective-permute-done.other_ref
  1.9 0.1 iota.7.place_ref
  2.0 1.8 %forecast.1 = f32[416,128]{1,0:T(8,128)} custom-call(f32[8,128]{1,0:T(8,128)S(1)} %iota.7.place_ref, f32[8,128]{1,0:T(8,128)S(1)} %get-tuple-element.14.kappa_ref, f32[1,5,16,256]{3,2,1,0:T(8,128)S(1)} %get-tuple-element.15.own_ref, f32[1,5,16,256]{3,2,1,0:T(8,128)S(1)} %collective-permute-done.other_ref, f32[2,16,256]{2,1,0:T(8,128)S(1)} %get-tuple-element.16.vel_own_ref, ...), custom_call_target="tpu_custom_call" | custom-call | tf_op jit(solution)/shard_map/forecast/pallas_call | solution.py:562
  3.8 8.8 %all-to-all-start = ((f32[16,26,1,128]{3,2,1,0:T(1,128)}), f32[16,26,1,128]{3,2,1,0:T(1,128)S(1)}, u32[]{:S(2)}, u32[]{:S(2)}) async-start(f32[16,26,1,128]{3,2,1,0:T(1,128)} %bitcast.5), calls=%async_computation | async-start | bytes 425984 | tf_op jit(solution)/shard_map/all_to_all | solution.py:574
  12.5 6.5 %localize.1 = (bf16[1024,1024]{1,0:T(8,128)(2,1)S(1)}, bf16[512,1024]{1,0:T(8,128)(2,1)S(1)}, bf16[512,1024]{1,0:T(8,128)(2,1)}, bf16[2048,256]{1,0:T(8,128)(2,1)}, bf16[2048,256]{1,0:T(8,128)(2,1)}) custom-call(f32[8,128]{1,0:T(8,128)S(1)} %iota.7.place_ref, f32[16,2048]{1,0:T(8,128)S(1)} %get-tuple-element.17.info_ref), custom_call_target="tpu_custom_call" | custom-call | tf_op jit(solution)/shard_map/localize/pallas_call | solution.py:585
  19.1 0.0 all-to-all-done
  19.1 5.3 %update.1 = f32[16,5,1,1,256]{4,3,2,1,0:T(1,128)} custom-call(f32[416,128]{1,0:T(8,128)S(1)} %bitcast.7, f32[16,2048]{1,0:T(8,128)S(1)} %get-tuple-element.17.info_ref, bf16[1024,1024]{1,0:T(8,128)(2,1)S(1)} %get-tuple-element.18.pair_hi_ref, bf16[512,1024]{1,0:T(8,128)(2,1)S(1)} %get-tuple-element.19.pair_lo_ref, ...), custom_call_target="tpu_custom_call" | custom-call | tf_op jit(solution)/shard_map/update/pallas_call | solution.py:608
  (1 shorter events, 0.0 us)
Async XLA Ops:
  0.0 1.9 %collective-permute-start.1 = (f32[2,16,256]{2,1,0:T(8,128)}, f32[2,16,256]{2,1,0:T(8,128)S(1)}, u32[]{:S(2)}, u32[]{:S(2)}) collective-permute-start(f32[2,16,256]{2,1,0:T(8,128)} %velocity_hbm.1), channel_id=1, source_target_pairs={{0,1},{1,0},{2,3},{3,2},{4,5},{5,4},{6,7},{7,6},{8,9},{9,8},{10,11... | collective-permute-start | bytes 98312 | tf_op jit(solution)/shard_map/ppermute | solution.py:528
  0.5 1.5 %collective-permute-start = (f32[1,5,16,256]{3,2,1,0:T(8,128)}, f32[1,5,16,256]{3,2,1,0:T(8,128)S(1)}, u32[]{:S(2)}, u32[]{:S(2)}) collective-permute-start(f32[1,5,16,256]{3,2,1,0:T(8,128)} %stack_hbm.1), channel_id=1, source_target_pairs={{0,1},{1,0},{2,3},{3,2},{4,5},{5,4},{6,7},{7,6},{8,9},{9,8},{10,11... | collective-permute-start | bytes 245768 | tf_op jit(solution)/shard_map/ppermute | solution.py:527
  3.8 15.3 %all-to-all-start = ((f32[16,26,1,128]{3,2,1,0:T(1,128)}), f32[16,26,1,128]{3,2,1,0:T(1,128)S(1)}, u32[]{:S(2)}, u32[]{:S(2)}) async-start(f32[16,26,1,128]{3,2,1,0:T(1,128)} %bitcast.5), calls=%async_computation | async-start | bytes 425984 | tf_op jit(solution)/shard_map/all_to_all | solution.py:574
